TPU v7x, 512 devices: a whole 4x8x8 slice. The times are simulated.
512 devices in a mesh: layer: 8 (over x, z_hi), row: 8 (over y), col: 8 (over z_lo, core).
Axes of the slice: x: 4, y: 8, z: 8 (z_hi: 2, z_lo: 4; z = z_hi * 4 + z_lo), core: 2. Of those that a mesh axis runs over, the one named last changes fastest.
Arguments:
- schur_window: float32 [4, 8, 256, 2, 8, 256], P(None, 'row', None, None, 'col'), may hold values from -8 to 24, as said below
Outputs:
- factored: float32 [4, 8, 256, 2, 8, 256], P(None, 'row', 'layer', None, 'col')
Inputs may be any that keep to these rules, and one draw needn't show every extreme that they name: `schur_window`: the leading 4096 columns of a symmetric positive definite matrix: its leading 4096 x 4096 block is symmetric and positive definite.
All inputs are finite; a program needn't handle non-finite values.
Results may differ from a plain program's by a relative error of at most 0.0001.
Values sent between devices are 32-bit elements; how exact they have to be, the bound alone decides.
No kernel may reach another device: no remote copies, remote signals or barrier semaphores. Data moves between devices by JAX's collectives and lax.ppermute only.
A program may use at most 64 MiB of HBM per device.

v0:
```python
import jax
import jax.numpy as jnp
from jax import lax
from jax.sharding import PartitionSpec as P

PANELS = 2


def picked(array, axis, root):
    return lax.dynamic_index_in_dim(lax.all_gather(array, axis), root, 0, keepdims=False)


def spread(array, axis, root):
    mine = lax.axis_index(axis) == root
    return lax.psum(jnp.where(mine, array, jnp.zeros_like(array)), axis)


def padded_to(lines, peers):
    spare = -len(lines) % peers
    return jnp.pad(lines, [(0, spare)] + [(0, 0)] * (lines.ndim - 1))


def broadcast_by_parts(array, axis, root):
    lines = jnp.where(lax.axis_index(axis) == root, array, jnp.zeros_like(array)).reshape(
        -1, *array.shape[1:][-1:]
    )
    padded = padded_to(lines, lax.axis_size(axis))
    own = lax.psum_scatter(padded, axis, scatter_dimension=0, tiled=True)
    return lax.all_gather(own, axis, axis=0, tiled=True)[: len(lines)].reshape(array.shape)


def in_blocks(array, dim, peers):
    before, after = (array.shape[:dim], array.shape[dim + 1 :])
    return jnp.moveaxis(array.reshape(*before, peers, -1, *after), dim, 0)


def sent_and_summed(array, axis, dim):
    peers = lax.axis_size(axis)
    pieces = lax.all_to_all(in_blocks(array, dim, peers), axis, 0, 0, tiled=True)
    return jnp.sum(pieces, axis=0)


def solve_rows(factor, column):
    block_count, panel_width, _ = column.shape
    flattened = column.reshape(block_count * panel_width, panel_width)
    solved = jax.scipy.linalg.solve_triangular(factor, flattened.T, lower=True)
    return solved.T.reshape(block_count, panel_width, panel_width)


def shape_panel(factor, solved, row_number, panel_index):
    row_marks = row_number[:, None, None]
    lower_rows = jnp.where(row_marks > panel_index, solved, jnp.zeros_like(solved))
    return jnp.where(row_marks == panel_index, factor[None], lower_rows)


def block_products(row_part, col_part):
    block_count, panel_width, _ = row_part.shape
    slot_count = col_part.shape[0]
    product = jnp.dot(
        row_part.reshape(block_count * panel_width, panel_width),
        col_part.reshape(slot_count * panel_width, panel_width).T,
        precision=lax.Precision.HIGHEST,
        preferred_element_type=jnp.float32,
    )
    return product.reshape(block_count, panel_width, slot_count, panel_width)


def add_slots(updates, row_part, col_part, active):

    def increase(current):
        return current + block_products(row_part, col_part)

    def unchanged(current):
        return current

    return lax.cond(active, increase, unchanged, updates)


def local(schur_window):
    row_blocks = schur_window.shape[0]
    panel_width = schur_window.shape[2]
    col_blocks = schur_window.shape[3]
    held_blocks = schur_window.reshape(row_blocks, panel_width, col_blocks, panel_width)
    grid_rows = lax.axis_size("row")
    grid_cols = lax.axis_size("col")
    layer_count = lax.axis_size("layer")
    layer_here = lax.axis_index("layer")
    col_here = lax.axis_index("col")
    row_number = jnp.arange(row_blocks, dtype=jnp.int32) * grid_rows + lax.axis_index("row")
    col_number = jnp.arange(col_blocks, dtype=jnp.int32) * grid_cols + col_here
    identity = jnp.eye(panel_width, dtype=jnp.float32)
    updates = jnp.zeros_like(held_blocks)
    for panel_index in range(PANELS):
        owner_col = panel_index % grid_cols
        owner_slot = panel_index // grid_cols
        pivot_row = panel_index % grid_rows
        pivot_slot = panel_index // grid_rows
        owner_layer = panel_index % layer_count
        column_here = held_blocks[:, :, owner_slot, :]
        if panel_index > 0:
            column_here = column_here - lax.psum(updates[:, :, owner_slot, :], "layer")
        pivot_here = column_here[pivot_slot]
        in_owner_col = col_here == owner_col
        pivot = picked(pivot_here, "row", pivot_row)
        factor = jnp.linalg.cholesky(jnp.where(in_owner_col, pivot, identity))
        panel_mine = shape_panel(factor, solve_rows(factor, column_here), row_number, panel_index)
        panel_rows = spread(panel_mine, "col", owner_col)
        pieces = []
        for col_slot in range(col_blocks):
            target = col_number[col_slot]
            source_slot = jnp.minimum(target // grid_rows, row_blocks - 1)
            piece = lax.dynamic_index_in_dim(panel_rows, source_slot, 0, keepdims=False)
            pieces.append(broadcast_by_parts(piece, "row", target % grid_rows))
        col_panel = jnp.stack(pieces)
        row_part = jnp.where(
            row_number[:, None, None] > panel_index, panel_rows, jnp.zeros_like(panel_rows)
        )
        col_part = jnp.where(
            col_number[:, None, None] > panel_index, col_panel, jnp.zeros_like(col_panel)
        )
        active = layer_here == owner_layer
        updates = add_slots(updates, row_part, col_part, active)
        kept_column = jnp.where(in_owner_col, panel_rows, held_blocks[:, :, owner_slot, :])
        held_blocks = held_blocks.at[:, :, owner_slot, :].set(kept_column)
    summed = sent_and_summed(updates, "layer", 1)
    share_rows = summed.shape[1]
    held_share = lax.dynamic_slice_in_dim(held_blocks, layer_here * share_rows, share_rows, 1)
    factored_cols = (col_number < PANELS)[None, None, :, None]
    upper_part = (row_number[:, None, None, None] < PANELS) & (
        col_number[None, None, :, None] > row_number[:, None, None, None]
    )
    result = jnp.where(factored_cols, held_share, held_share - summed)
    result = jnp.where(upper_part, jnp.zeros_like(result), result)
    return result.reshape(row_blocks, 1, share_rows, col_blocks, 1, panel_width)


def solution(mesh):
    return jax.shard_map(
        local,
        mesh=mesh,
        in_specs=(P(None, "row", None, None, "col", None),),
        out_specs=P(None, "row", "layer", None, "col", None),
        check_vma=False,
    )
```

profile of v0, /device:TPU:64, one launch (start us, length us, event | category | flops | bytes accessed | tf_op | source)
XLA Modules:
  0.0 830.9 jit_solution(384619336028586609)
XLA Ops:
  6.5 1.8 copy.102
  9.2 1.0 slice.138
  10.2 1.6 copy.68
  11.8 44.9 %all-gather.6.cloned.1.call-done = f32[8,256,1,256]{3,1,2,0:T(8,128)} async-done(((f32[1,256,1,256]{3,1,2,0:T(8,128)}), f32[8,256,1,256]{3,1,2,0:T(8,128)}) %all-gather.6.cloned.1.call-update) | async-done | bytes 2097168 | tf_op jit(solution)/shard_map/all_gather | solution.py:10
  56.7 1.0 slice.137
  58.1 11.7 %cholesky.130 = f32[128,128]{1,0:T(8,128)S(1)} custom-call(f32[128,128]{1,0:T(8,128)S(1)} %cholesky.194), custom_call_target="Cholesky" | custom-call | tf_op jit(solution)/shard_map/jit(cholesky)/cholesky | solution.py:105
  69.8 9.8 %custom-call.13 = f32[1,128,128]{1,2,0:T(8,128)S(1)} custom-call(f32[1,128,128]{2,1,0:T(8,128)S(1)} %get-tuple-element.173), custom_call_target="InvertDiagBlocksLowerTriangular" | custom-call | tf_op jit(solution)/shard_map/jit(cholesky)/cholesky | solution.py:105
  80.1 11.7 %cholesky.147 = f32[128,128]{1,0:T(8,128)S(1)} custom-call(f32[128,128]{1,0:T(8,128)S(1)} %convolution_subtract_fusion.3), custom_call_target="Cholesky" | custom-call | tf_op jit(solution)/shard_map/jit(cholesky)/cholesky | solution.py:105
  93.9 4.0 while.6
  94.6 1.3 bitcast_dynamic-update-slice_fusion.6
  96.5 1.3 bitcast_dynamic-update-slice_fusion.6
  98.4 19.7 %custom-call.14 = f32[2,128,128]{1,2,0:T(8,128)S(1)} custom-call(f32[2,128,128]{2,1,0:T(8,128)S(1)} %get-tuple-element.104), custom_call_target="InvertDiagBlocksLowerTriangular" | custom-call | tf_op jit(solution)/shard_map/jit(_solve_triangular)/triangular_solve | solution.py:46
  120.4 1.2 select_select_fusion.1
  127.0 71.2 %all-reduce.5.cloned.1.call-done = f32[4,256,256]{2,1,0:T(8,128)} async-done(((f32[4,256,256]{2,1,0:T(8,128)}), f32[4,256,256]{2,1,0:T(8,128)}) %all-reduce.5.cloned.1.call-update) | async-done | bytes 1048592 | tf_op jit(solution)/shard_map/psum | solution.py:15
  198.2 1.8 select_bitcast_fusion.3
  200.7 41.5 %reduce-scatter.13.cloned.1.call-done = f32[32,256]{1,0:T(8,128)} async-done(((f32[256,256]{1,0:T(8,128)}), f32[32,256]{1,0:T(8,128)}) %reduce-scatter.13.cloned.1.call-update) | async-done | bytes 32784 | tf_op jit(solution)/shard_map/reduce_scatter | solution.py:28
  242.2 25.0 %all_gather.19 = f32[256,256]{1,0:T(8,128)S(1)} all-gather(f32[32,256]{1,0:T(8,128)} %reduce-scatter.13.cloned.1.call-done), channel_id=1, replica_groups=mesh['layer'=8,'row'=8,'col'=8] {'row'}, dimensions={0}, use_global_device_ids=true | all-gather | bytes 294912 | tf_op jit(solution)/shard_map/all_gather | solution.py:29
  267.2 16.2 %reduce-scatter.15.cloned.1.call-done = f32[32,256]{1,0:T(8,128)} async-done(((f32[256,256]{1,0:T(8,128)}), f32[32,256]{1,0:T(8,128)}) %reduce-scatter.15.cloned.1.call-update) | async-done | bytes 32784 | tf_op jit(solution)/shard_map/reduce_scatter | solution.py:28
  283.4 25.0 %all_gather.20 = f32[256,256]{1,0:T(8,128)S(1)} all-gather(f32[32,256]{1,0:T(8,128)} %reduce-scatter.15.cloned.1.call-done), channel_id=1, replica_groups=mesh['layer'=8,'row'=8,'col'=8] {'row'}, dimensions={0}, use_global_device_ids=true | all-gather | bytes 294912 | tf_op jit(solution)/shard_map/all_gather | solution.py:29
  308.4 0.8 pad_maximum_fusion
  309.4 1.1 broadcast.308
  310.5 0.8 broadcast.312
  311.3 3.5 conditional.2
  311.3 3.5 fusion
  314.8 1.1 slice_bitcast_fusion
  315.9 133.5 %all-reduce.7.cloned.1.call-done = f32[4,256,256]{2,1,0:T(8,128)} async-done(((f32[4,256,256]{2,1,0:T(8,128)}), f32[4,256,256]{2,1,0:T(8,128)}) %all-reduce.7.cloned.1.call-update) | async-done | bytes 1048592 | tf_op jit(solution)/shard_map/psum | solution.py:101
  449.5 1.8 fusion.31
  451.3 1.0 copy-done.4
  453.3 2.6 copy.77
  455.9 38.1 %all-gather.4.cloned.1.call-done = f32[8,256,256]{2,1,0:T(8,128)} async-done(((f32[1,256,256]{2,1,0:T(8,128)}), f32[8,256,256]{2,1,0:T(8,128)}) %all-gather.4.cloned.1.call-update) | async-done | bytes 2097168 | tf_op jit(solution)/shard_map/all_gather | solution.py:10
  494.0 1.7 dynamic_slice.30
  495.7 1.1 copy.100
  497.5 1.8 copy.76
  499.3 1.0 fusion.17
  501.0 11.7 %cholesky.164 = f32[128,128]{1,0:T(8,128)S(1)} custom-call(f32[128,128]{1,0:T(8,128)S(1)} %cholesky.197), custom_call_target="Cholesky" | custom-call | tf_op jit(solution)/shard_map/jit(cholesky)/cholesky | solution.py:105
  512.8 9.8 %custom-call.15 = f32[1,128,128]{1,2,0:T(8,128)S(1)} custom-call(f32[1,128,128]{2,1,0:T(8,128)S(1)} %get-tuple-element.169), custom_call_target="InvertDiagBlocksLowerTriangular" | custom-call | tf_op jit(solution)/shard_map/jit(cholesky)/cholesky | solution.py:105
  522.6 1.0 constant_dynamic-update-slice_fusion
  523.6 1.1 convolution_subtract_fusion.2
  524.7 11.7 %cholesky.181 = f32[128,128]{1,0:T(8,128)S(1)} custom-call(f32[128,128]{1,0:T(8,128)S(1)} %convolution_subtract_fusion.2), custom_call_target="Cholesky" | custom-call | tf_op jit(solution)/shard_map/jit(cholesky)/cholesky | solution.py:105
  539.0 1.7 fusion.19
  540.7 5.3 while.7
  542.2 1.3 bitcast_dynamic-update-slice_fusion.7
  544.7 1.3 bitcast_dynamic-update-slice_fusion.7
  546.6 20.5 %custom-call.16 = f32[2,128,128]{1,2,0:T(8,128)S(1)} custom-call(f32[2,128,128]{2,1,0:T(8,128)} %copy-done.8), custom_call_target="InvertDiagBlocksLowerTriangular" | custom-call | tf_op jit(solution)/shard_map/jit(_solve_triangular)/triangular_solve | solution.py:46
  567.1 1.7 fusion.11
  568.8 1.6 convolution_subtract_fusion
  571.1 1.1 maximum_bitcast_fusion.1
  572.1 2.5 copy.78
  574.7 2.4 select_select_fusion
  577.1 76.7 %all-reduce.9.cloned.1.call-done = f32[4,256,256]{2,1,0:T(8,128)} async-done(((f32[4,256,256]{2,1,0:T(8,128)}), f32[4,256,256]{2,1,0:T(8,128)}) %all-reduce.9.cloned.1.call-update) | async-done | bytes 1048592 | tf_op jit(solution)/shard_map/psum | solution.py:15
  653.8 1.9 select_bitcast_fusion.1
  656.5 41.3 %reduce-scatter.17.cloned.1.call-done = f32[32,256]{1,0:T(8,128)} async-done(((f32[256,256]{1,0:T(8,128)}), f32[32,256]{1,0:T(8,128)}) %reduce-scatter.17.cloned.1.call-update) | async-done | bytes 32784 | tf_op jit(solution)/shard_map/reduce_scatter | solution.py:28
  697.8 25.0 %all_gather.22 = f32[256,256]{1,0:T(8,128)S(1)} all-gather(f32[32,256]{1,0:T(8,128)} %reduce-scatter.17.cloned.1.call-done), channel_id=1, replica_groups=mesh['layer'=8,'row'=8,'col'=8] {'row'}, dimensions={0}, use_global_device_ids=true | all-gather | bytes 294912 | tf_op jit(solution)/shard_map/all_gather | solution.py:29
  722.8 16.4 %reduce-scatter.19.cloned.1.call-done = f32[32,256]{1,0:T(8,128)} async-done(((f32[256,256]{1,0:T(8,128)}), f32[32,256]{1,0:T(8,128)}) %reduce-scatter.19.cloned.1.call-update) | async-done | bytes 32784 | tf_op jit(solution)/shard_map/reduce_scatter | solution.py:28
  739.2 25.0 %all_gather.23 = f32[256,256]{1,0:T(8,128)S(1)} all-gather(f32[32,256]{1,0:T(8,128)} %reduce-scatter.19.cloned.1.call-done), channel_id=1, replica_groups=mesh['layer'=8,'row'=8,'col'=8] {'row'}, dimensions={0}, use_global_device_ids=true | all-gather | bytes 294912 | tf_op jit(solution)/shard_map/all_gather | solution.py:29
  764.2 0.9 pad_maximum_fusion.1
  765.2 1.5 copy.84
  766.7 10.9 %all-to-all-start = ((f32[8,4,32,2,256]{4,2,3,1,0:T(8,128)}), f32[8,4,32,2,256]{4,2,3,1,0:T(8,128)}, u32[]{:S(2)}, u32[]{:S(2)}) async-start(f32[8,4,32,2,256]{4,2,3,1,0:T(8,128)} %copy.84), calls=%async_computation | async-start | bytes 4194304 | tf_op jit(solution)/shard_map/all_to_all | solution.py:39
  777.8 1.6 copy.79
  779.4 1.1 bitcast_dynamic-update-slice_fusion.2
  780.5 39.6 %all-to-all-done = f32[8,4,32,2,256]{4,2,3,1,0:T(8,128)} async-done(((f32[8,4,32,2,256]{4,2,3,1,0:T(8,128)}), f32[8,4,32,2,256]{4,2,3,1,0:T(8,128)}, u32[]{:S(2)}, u32[]{:S(2)}) %all-to-all-start) | async-done | bytes 2097184 | tf_op jit(solution)/shard_map/all_to_all | solution.py:39
  820.1 1.8 reduce_sum.9
  821.9 1.1 fusion.16
  823.0 1.0 copy.86
  (90 shorter events, 16.6 us)
Async XLA Ops:
  6.5 50.2 %all-gather.6.cloned.1.call-start = ((), (), s32[]{:S(2)}) async-start(), calls=%async_computation.9 | async-start | bytes 2359296 | tf_op jit(solution)/shard_map/all_gather | solution.py:10
  8.3 3.5 copy-start
  9.1 189.1 %all-reduce.5.cloned.1.call-start = ((), (), s32[]{:S(2)}) async-start(), calls=%async_computation.5 | async-start | bytes 2097152 | tf_op jit(solution)/shard_map/psum | solution.py:15
  97.8 0.5 copy-start.9
  121.6 120.6 %reduce-scatter.13.cloned.1.call-start = ((), (), s32[]{:S(2)}) async-start(), calls=%async_computation.10 | async-start | bytes 294912 | tf_op jit(solution)/shard_map/reduce_scatter | solution.py:28
  200.1 111.3 %copy-start.2 = (f32[4,256,256]{2,1,0:T(8,128)S(1)}, f32[4,256,256]{2,1,0:T(8,128)}, u32[]{:S(2)}) copy-start(f32[4,256,256]{2,1,0:T(8,128)} %all-reduce.5.cloned.1.call-done) | copy-start | bytes 3145732
  200.1 83.4 %reduce-scatter.15.cloned.1.call-start = ((), (), s32[]{:S(2)}) async-start(), calls=%async_computation.11 | async-start | bytes 294912 | tf_op jit(solution)/shard_map/reduce_scatter | solution.py:28
  200.7 248.8 %all-reduce.7.cloned.1.call-start = ((), (), s32[]{:S(2)}) async-start(), calls=%async_computation.6 | async-start | bytes 2097152 | tf_op jit(solution)/shard_map/psum | solution.py:101
  315.9 178.1 %all-gather.4.cloned.1.call-start = ((), (), s32[]{:S(2)}) async-start(), calls=%async_computation.7 | async-start | bytes 2359296 | tf_op jit(solution)/shard_map/all_gather | solution.py:10
  451.3 1.0 copy-start.4
  453.1 200.8 %all-reduce.9.cloned.1.call-start = ((), (), s32[]{:S(2)}) async-start(), calls=%async_computation.8 | async-start | bytes 2097152 | tf_op jit(solution)/shard_map/psum | solution.py:15
  500.3 0.7 copy-start.7
  536.5 2.5 copy-start.6
  546.0 0.6 copy-start.8
  571.1 3.6 copy-start.5
  577.1 120.7 %reduce-scatter.17.cloned.1.call-start = ((), (), s32[]{:S(2)}) async-start(), calls=%async_computation.12 | async-start | bytes 294912 | tf_op jit(solution)/shard_map/reduce_scatter | solution.py:28
  655.7 83.5 %reduce-scatter.19.cloned.1.call-start = ((), (), s32[]{:S(2)}) async-start(), calls=%async_computation.13 | async-start | bytes 294912 | tf_op jit(solution)/shard_map/reduce_scatter | solution.py:28
  766.7 11.0 %copy-start.1 = (f32[4,1,256,2,1,256]{5,2,0,3,4,1:T(8,128)S(1)}, f32[4,1,256,2,1,256]{5,2,0,3,4,1:T(8,128)}, u32[]{:S(2)}) copy-start(f32[4,1,256,2,1,256]{5,2,0,3,4,1:T(8,128)} %copy-done) | copy-start | bytes 6291460
  766.7 53.4 %all-to-all-start = ((f32[8,4,32,2,256]{4,2,3,1,0:T(8,128)}), f32[8,4,32,2,256]{4,2,3,1,0:T(8,128)}, u32[]{:S(2)}, u32[]{:S(2)}) async-start(f32[8,4,32,2,256]{4,2,3,1,0:T(8,128)} %copy.84), calls=%async_computation | async-start | bytes 4194304 | tf_op jit(solution)/shard_map/all_to_all | solution.py:39
  777.8 1.6 copy-start.3
Sparse Core Ops, SparseCore 0:
  9.4 47.2 all-gather.5
  121.7 76.4 all-reduce.4
  201.0 41.1 reduce-scatter.12
  244.8 38.5 reduce-scatter.14
  316.0 133.4 all-reduce.6
  453.2 40.7 all-gather.3
  577.2 76.5 all-reduce.8
  656.6 41.1 reduce-scatter.16
  700.6 38.5 reduce-scatter.18
where the time goes:
time: 840 us; the launch traced here: 831 us
  waiting for transfers between devices  521 us (62%)
  other arithmetic  128 us (15%)
  blocking collectives  100 us (12%)
  local copies, waits for them, and re-layouts  36.7 us (4%)
  between operations  21.3 us (3%)
  matrix products  11.8 us (1%)
  starting transfers between devices  11.4 us (1%)
    psum x2, waiting for transfers between devices, spread(): return lax.psum(jnp.where(mine, array, jnp.zeros_like(array)), axis)  148 us
    psum x1, waiting for transfers between devices, local(): column_here = column_here - lax.psum(updates[:, :, owner_slot, :], 'layer')  134 us
    reduce_scatter x4, waiting for transfers between devices, broadcast_by_parts(): own = lax.psum_scatter(padded, axis, scatter_dimension=0, tiled=True)  115 us
    all_gather x4, blocking collectives, broadcast_by_parts(): lax.all_gather(own, axis, axis=0, tiled=True)[:len(lines)]  100 us
    all_gather x2, waiting for transfers between devices, picked(): lax.all_gather(array, axis)  83 us
    another operation x13, other arithmetic, local(): factor = jnp.linalg.cholesky(jnp.where(in_owner_col, pivot, identity))  68.5 us
    another operation x5, other arithmetic, solve_rows(): solved = jax.scipy.linalg.solve_triangular(factor, flattened.T, lower=True)  41.9 us
    all_to_all x1, waiting for transfers between devices, sent_and_summed(): lax.all_to_all(in_blocks(array, dim, peers), axis, 0, 0, tiled=True)  39.6 us
  transfers between devices with their start and end apart: 10, of which 10 were waited for; matrix products, arithmetic and copies ran while one was open for 1% of the time, Pallas kernels for 0%

commit v1 on v0

v1 whole, which is shorter than its diff:
```python
import jax
import jax.numpy as jnp
from jax import lax
from jax.experimental import pallas as pl
from jax.experimental.pallas import tpu as pltpu
from jax.sharding import PartitionSpec as P

PANELS = 2
BLOCK = 128
STRIP = 32
HIGHEST = lax.Precision.HIGHEST


def product(left, right, dims=((1,), (0,))):
    return lax.dot_general(
        left, right, (dims, ((), ())), precision=HIGHEST, preferred_element_type=jnp.float32
    )


def eliminate(groups, first_lane):
    group_count = len(groups)
    sublane = lax.broadcasted_iota(jnp.int32, (8, 128), 0)
    parts = [[group[:, :128], group[:, 128:]] for group in groups]
    finished = []
    for g in range(group_count):
        lane = first_lane + 8 * g
        heads = [
            [jnp.broadcast_to(parts[i][0][:, lane + s : lane + s + 1], (8, 128)) for s in range(8)]
            for i in range(g, group_count)
        ]
        scale = None
        for s in range(8):
            root = lax.rsqrt(jnp.broadcast_to(heads[0][s][s : s + 1, :], (8, 128)))
            inverse = root * root
            scale = root if s == 0 else jnp.where(sublane == s, root, scale)
            rows = [jnp.broadcast_to(part[s : s + 1, :], (8, 128)) for part in parts[g]]
            head_rows = [
                jnp.broadcast_to(heads[0][p][s : s + 1, :], (8, 128)) for p in range(s + 1, 8)
            ]
            for i in range(g, group_count):
                factor = heads[i - g][s] * inverse
                if i == g:
                    if s == 7:
                        continue
                    factor = jnp.where(sublane > s, factor, 0.0)
                for w in range(2):
                    parts[i][w] = parts[i][w] - factor * rows[w]
                for p in range(s + 1, 8):
                    heads[i - g][p] = heads[i - g][p] - factor * head_rows[p - s - 1]
        finished.append([part * scale for part in parts[g]])
    return [jnp.concatenate([rows[w] for rows in finished], axis=0) for w in range(2)]


def factor_kernel(a_ref, e_ref, work_ref, block_ref):
    size = a_ref.shape[0]
    block_count = size // BLOCK
    work_ref[...] = a_ref[...]
    e_ref[...] = jnp.zeros_like(e_ref)
    row_id = lax.broadcasted_iota(jnp.int32, (BLOCK, BLOCK), 0)
    col_id = lax.broadcasted_iota(jnp.int32, (BLOCK, BLOCK), 1)
    identity = (row_id == col_id).astype(jnp.float32)
    for k in range(block_count):
        begin, end = k * BLOCK, (k + 1) * BLOCK
        block_ref[:, :BLOCK] = work_ref[begin:end, begin:end]
        block_ref[:, BLOCK:] = identity
        for first in range(0, BLOCK, STRIP):
            last = first + STRIP
            groups = [block_ref[first + 8 * i : first + 8 * i + 8, :] for i in range(STRIP // 8)]
            done = eliminate(groups, first)
            both = jnp.concatenate(done, axis=1)
            block_ref[first:last, :] = both
            if last < BLOCK:
                block_ref[last:, :] -= product(done[0].T[last:], both)
        inverse = block_ref[:, BLOCK:]
        e_ref[begin:end, begin:end] = inverse
        if end < size:
            upper = product(inverse, work_ref[begin:end, end:])
            lower = upper.T
            work_ref[end:, end:] -= product(lower, upper)
        if begin > 0:
            e_ref[begin:end, :begin] = product(inverse, e_ref[begin:end, :begin])
        if end < size:
            e_ref[end:, :end] -= product(lower, e_ref[begin:end, :end])


def inverse_factor(matrix):
    size = matrix.shape[0]
    return pl.pallas_call(
        factor_kernel,
        out_shape=jax.ShapeDtypeStruct((size, size), jnp.float32),
        scratch_shapes=[
            pltpu.VMEM((size, size), jnp.float32),
            pltpu.VMEM((BLOCK, 2 * BLOCK), jnp.float32),
        ],
        name="factor",
    )(matrix)


def to_all(piece, axis, peers, groups=None):
    copies = jnp.broadcast_to(piece[None], (peers, *piece.shape))
    return lax.all_to_all(copies, axis, 0, 0, axis_index_groups=groups)


def local(schur_window):
    row_blocks, _, width, col_blocks, _, _ = schur_window.shape
    held = schur_window.reshape(row_blocks, width, col_blocks, width)
    layers = lax.axis_size("layer")
    grid_rows = lax.axis_size("row")
    grid_cols = lax.axis_size("col")
    layer_here = lax.axis_index("layer")
    row_here = lax.axis_index("row")
    col_here = lax.axis_index("col")
    x_size = layers // 2
    x_groups = [[x * 2 + z for x in range(x_size)] for z in range(2)]
    share = width // layers
    quarter = width // x_size
    lead = PANELS * width

    head = lax.dynamic_slice_in_dim(held[0], (layer_here // 2) * quarter, quarter, 0)
    quarters = to_all(head, "row", grid_rows)[:PANELS]
    gathered = to_all(quarters, "layer", x_size, x_groups)
    top = jnp.moveaxis(gathered, 0, 1).reshape(lead, col_blocks, width)

    mine = lax.dynamic_slice_in_dim(held, layer_here * share, share, 1)
    mine_first = mine[:, :, 0, :].reshape(row_blocks * share, width)
    swapped_in = jnp.concatenate([top[:, 0, :], mine_first], axis=0)
    swapped = lax.ppermute(swapped_in, "col", [(0, 1), (1, 0)])
    is_first = col_here == 0
    both = jnp.concatenate(
        [jnp.where(is_first, swapped_in, swapped), jnp.where(is_first, swapped, swapped_in)], axis=1
    )
    inverse = inverse_factor(both[:lead])
    solved = product(both[lead:], inverse, ((1,), (1,)))
    weights = product(solved, inverse)

    half = lax.dynamic_slice_in_dim(weights, (col_here % 2) * width, width, 1)
    far = lax.ppermute(half, "col", [(0, 4), (1, 5)])
    half = jnp.where(col_here < 4, half, far)
    near = lax.ppermute(half, "col", [(0, 2), (1, 3), (4, 6), (5, 7)])
    half = jnp.where(col_here % 4 < 2, half, near)
    other = lax.ppermute(half, "col", [(i, i ^ 1) for i in range(grid_cols)])
    is_even = col_here % 2 == 0
    weights_here = jnp.concatenate(
        [jnp.where(is_even, half, other), jnp.where(is_even, other, half)], axis=1
    )
    update = product(weights_here, top.reshape(lead, col_blocks * width))
    trailing = mine - update.reshape(row_blocks, share, col_blocks, width)

    row_number = (jnp.arange(row_blocks, dtype=jnp.int32) * grid_rows + row_here)[:, None, None, None]
    col_number = (jnp.arange(col_blocks, dtype=jnp.int32) * grid_cols + col_here)[None, None, :, None]
    row_inside = (jnp.arange(share, dtype=jnp.int32) + layer_here * share)[None, :, None, None]
    col_inside = jnp.arange(width, dtype=jnp.int32)[None, None, None, :]
    panel = jnp.where(is_first, solved[:, :width], solved[:, width : 2 * width])
    panel = panel.reshape(row_blocks, share, 1, width)
    below = (row_number > col_number) | ((row_number == col_number) & (row_inside >= col_inside))
    panel = jnp.where(below, panel, 0.0)
    trailing = jnp.where(row_number < PANELS, 0.0, trailing)
    result = jnp.where(col_number < PANELS, panel, trailing)
    return result.reshape(row_blocks, 1, share, col_blocks, 1, width)


def solution(mesh):
    return jax.shard_map(
        local,
        mesh=mesh,
        in_specs=(P(None, "row", None, None, "col", None),),
        out_specs=P(None, "row", "layer", None, "col", None),
        check_vma=False,
    )
```

time: 840 us -> 106 us (0.13)
  the two profiles are of different devices: /device:TPU:64 before, /device:TPU:1 now
where the time goes in v1:
time: 106 us; the launch traced here: 105 us
  blocking collectives  33.5 us (32%)
  Pallas kernels  21.1 us (20%)
  starting transfers between devices  19.2 us (18%)
  waiting for transfers between devices  17.7 us (17%)
  local copies, waits for them, and re-layouts  6.08 us (6%)
  matrix products  4.56 us (4%)
  other arithmetic  2.61 us (2%)
    all_to_all x1, blocking collectives, to_all(): return lax.all_to_all(copies, axis, 0, 0, axis_index_groups=groups)  33.5 us
    pallas_call x1, Pallas kernels, inverse_factor(): pl.pallas_call(factor_kernel, out_shape=jax.ShapeDtypeStruct((size, size)...  21.1 us
    all_to_all x1, waiting for transfers between devices, to_all(): return lax.all_to_all(copies, axis, 0, 0, axis_index_groups=groups)  11.1 us
    ppermute x1, starting transfers between devices, local(): other = lax.ppermute(half, 'col', [(i, i ^ 1) for i in range(grid_cols)])  5.7 us
    ppermute x1, starting transfers between devices, local(): swapped = lax.ppermute(swapped_in, 'col', [(0, 1), (1, 0)])  5.68 us
    all_to_all x1, starting transfers between devices, to_all(): return lax.all_to_all(copies, axis, 0, 0, axis_index_groups=groups)  5.28 us
    dot_general x3, matrix products, product(): lax.dot_general(left, right, (dims, ((), ())), precision=HIGHEST, preferr...  4.56 us
  transfers between devices with their start and end apart: 5, of which 5 were waited for; matrix products, arithmetic and copies ran while one was open for 2% of the time, Pallas kernels for 0%

profile of v1, /device:TPU:1, one launch (start us, length us, event | category | flops | bytes accessed | tf_op | source)
XLA Modules:
  0.0 105.1 jit_solution(11738054310464559562)
XLA Ops:
  0.0 1.4 %slice.25 = f32[1,1,256,2,1,256]{5,4,3,2,1,0:T(1,128)S(1)} slice(f32[4,1,256,2,1,256]{5,4,3,2,1,0:T(1,128)} %param.1), slice={[0:1], [0:1], [0:256], [0:2], [0:1], [0:256]} | slice | bytes 1048576 | tf_op jit(solution)/shard_map/slice | solution.py:119
  1.5 0.1 copy.11
  1.6 0.3 broadcast_in_dim.52
  1.8 33.5 %all_to_all.10 = f32[8,64,2,256]{3,2,1,0:T(2,128)S(1)} all-to-all(f32[8,64,2,256]{3,2,1,0:T(2,128)S(1)} %broadcast_in_dim.52), channel_id=1, replica_groups=mesh['layer'=8,'row'=8,'col'=8] {'row'}, dimensions={0} | all-to-all | bytes 2097152 | tf_op jit(solution)/shard_map/all_to_all | solution.py:101
  35.4 1.2 %broadcast_in_dim.53 = f32[4,2,64,2,256]{4,3,2,1,0:T(2,128)} broadcast(f32[2,64,2,256]{3,2,1,0:T(2,128)S(1)} %slice.33), dimensions={1,2,3,4} | broadcast | bytes 1310720 | tf_op jit(solution)/shard_map/broadcast_in_dim | solution.py:100
  36.6 5.3 %all-to-all-start.1 = ((f32[4,2,64,2,256]{4,3,2,1,0:T(2,128)}), f32[4,2,64,2,256]{4,3,2,1,0:T(2,128)S(1)}, u32[]{:S(2)}, u32[]{:S(2)}) async-start(f32[4,2,64,2,256]{4,3,2,1,0:T(2,128)} %broadcast_in_dim.53), calls=%async_computation.1 | async-start | bytes 2097152 | tf_op jit(solution)/shard_map/all_to_all | solution.py:101
  41.9 1.1 %constant_dynamic-slice_fusion.1 = f32[4,1,32,2,1,256]{5,4,3,2,1,0:T(1,128)S(1)} fusion(f32[4,1,256,2,1,256]{5,4,3,2,1,0:T(1,128)} %param.1, s32[]{:T(128)S(6)} %select_n.84), kind=kLoop, calls=%fused_computation.25 | loop fusion | bytes 524292 | tf_op jit(solution)/shard_map/dynamic_slice | solution.py:124
  43.0 11.1 %all-to-all-done.1 = f32[4,2,64,2,256]{4,3,2,1,0:T(2,128)S(1)} async-done(((f32[4,2,64,2,256]{4,3,2,1,0:T(2,128)}), f32[4,2,64,2,256]{4,3,2,1,0:T(2,128)S(1)}, u32[]{:S(2)}, u32[]{:S(2)}) %all-to-all-start.1) | async-done | bytes 1048608 | tf_op jit(solution)/shard_map/all_to_all | solution.py:101
  54.2 0.1 copy.12
  54.4 5.7 %collective-permute-start = (f32[640,256]{1,0:T(8,128)S(1)}, f32[640,256]{1,0:T(8,128)}, u32[]{:S(2)}, u32[]{:S(2)}) collective-permute-start(f32[640,256]{1,0:T(8,128)S(1)} %pad_maximum_fusion.1), channel_id=1, source_target_pairs={{0,1},{1,0},{8,9},{9,8},{16,17},{17,16},{24,25},{25,24},{32,33},{3... | collective-permute-start | bytes 1966088 | tf_op jit(solution)/shard_map/ppermute | solution.py:127
  60.1 0.1 iota_compare_fusion
  60.2 1.7 %collective-permute-done = f32[640,256]{1,0:T(8,128)} collective-permute-done((f32[640,256]{1,0:T(8,128)S(1)}, f32[640,256]{1,0:T(8,128)}, u32[]{:S(2)}, u32[]{:S(2)}) %collective-permute-start) | collective-permute-done | bytes 655392 | tf_op jit(solution)/shard_map/ppermute | solution.py:127
  61.9 1.2 %broadcast_select_fusion.1 = (f32[640,256]{1,0:T(8,128)S(1)}, f32[640,256]{1,0:T(8,128)S(1)}) fusion(f32[640,256]{1,0:T(8,128)} %collective-permute-done, pred[]{:T(512)S(6)} %eq.25, f32[128,256]{1,0:T(8,128)S(1)} %bitcast.41, f32[512,256]{1,0:T(8,128)S(1)} %slice_bitcast_fusion), kind=kLoop, calls=%fused_computation.8 | loop fusion | flops 491520 | bytes 2621441 | tf_op jit(solution)/shard_map/jit(_where)/select_n | solution.py:130
  63.1 1.1 %pad_maximum_fusion.a_ref = f32[512,512]{1,0:T(8,128)} fusion(f32[640,256]{1,0:T(8,128)S(1)} %get-tuple-element.6, f32[640,256]{1,0:T(8,128)S(1)} %get-tuple-element.5), kind=kLoop, calls=%fused_computation.4 | loop fusion | flops 262144 | bytes 2359296 | tf_op jit(solution)/shard_map/concatenate | solution.py:129
  64.2 21.1 %factor.1 = f32[512,512]{1,0:T(8,128)} custom-call(f32[512,512]{1,0:T(8,128)} %pad_maximum_fusion.a_ref), custom_call_target="tpu_custom_call" | custom-call | tf_op jit(solution)/shard_map/factor/pallas_call | solution.py:88
  85.3 0.0 copy-start
  85.3 2.5 %fusion.3 = f32[128,512]{1,0:T(8,128)S(1)} fusion(f32[512,512]{1,0:T(8,128)} %factor.1, f32[640,256]{1,0:T(8,128)S(1)} %get-tuple-element.6, f32[640,256]{1,0:T(8,128)S(1)} %get-tuple-element.5), kind=kOutput, calls=%fused_computation.9 | convolution fusion | flops 402718720 | bytes 2621440 | tf_op jit(solution)/shard_map/dot_general | solution.py:15
  87.8 0.0 copy-done
  87.8 0.9 fusion.8
  88.8 1.3 %collective-permute-start.1 = (f32[128,256]{1,0:T(8,128)S(1)}, f32[128,256]{1,0:T(8,128)S(1)}, u32[]{:S(2)}, u32[]{:S(2)}) collective-permute-start(f32[128,256]{1,0:T(8,128)S(1)} %constant_dynamic-slice_fusion), channel_id=1, source_target_pairs={{0,4},{1,5},{8,12},{9,13},{16,20},{17,21},{24,28},{25,29},{32,36},... | collective-permute-start | bytes 393224 | tf_op jit(solution)/shard_map/ppermute | solution.py:137
  90.1 0.1 broadcast_compare_fusion.1
  90.2 1.8 %collective-permute-done.1 = f32[128,256]{1,0:T(8,128)S(1)} collective-permute-done((f32[128,256]{1,0:T(8,128)S(1)}, f32[128,256]{1,0:T(8,128)S(1)}, u32[]{:S(2)}, u32[]{:S(2)}) %collective-permute-start.1) | collective-permute-done | bytes 131104 | tf_op jit(solution)/shard_map/ppermute | solution.py:137
  92.0 1.3 %collective-permute-start.2 = (f32[128,256]{1,0:T(8,128)S(1)}, f32[128,256]{1,0:T(8,128)S(1)}, u32[]{:S(2)}, u32[]{:S(2)}) collective-permute-start(f32[128,256]{1,0:T(8,128)S(1)} %broadcast_select_fusion.2), channel_id=1, source_target_pairs={{0,2},{1,3},{4,6},{5,7},{8,10},{9,11},{12,14},{13,15},{16,18},{17,... | collective-permute-start | bytes 393224 | tf_op jit(solution)/shard_map/ppermute | solution.py:139
  93.4 0.4 copy.14
  93.8 0.1 copy.20
  93.8 0.3 copy.15
  94.2 2.0 %collective-permute-done.2 = f32[128,256]{1,0:T(8,128)S(1)} collective-permute-done((f32[128,256]{1,0:T(8,128)S(1)}, f32[128,256]{1,0:T(8,128)S(1)}, u32[]{:S(2)}, u32[]{:S(2)}) %collective-permute-start.2) | collective-permute-done | bytes 131104 | tf_op jit(solution)/shard_map/ppermute | solution.py:139
  96.2 5.7 %collective-permute-start.3 = (f32[128,256]{1,0:T(8,128)S(1)}, f32[128,256]{1,0:T(8,128)S(1)}, u32[]{:S(2)}, u32[]{:S(2)}) collective-permute-start(f32[128,256]{1,0:T(8,128)S(1)} %broadcast_select_fusion.3), channel_id=1, source_target_pairs={{0,1},{1,0},{2,3},{3,2},{4,5},{5,4},{6,7},{7,6},{8,9},{9,8},{10,11... | collective-permute-start | bytes 393224 | tf_op jit(solution)/shard_map/ppermute | solution.py:141
  102.0 0.9 collective-permute-done.3
  102.9 1.2 %fusion.2 = f32[4,1,32,2,1,256]{5,2,3,0,4,1:T(8,128)S(1)} fusion(f32[4,32,512,1]{2,1,3,0:T(8,128)S(1)} %bitcast.42, f32[2,256,512,1]{2,1,0,3:T(8,128)S(1)} %bitcast.36, f32[4,32,256]{2,1,0:T(8,128)S(1)} %bitcast.44, pred[4]{0:T(512)(128)(4,1)S(1)} %broadcast_compare_fusion.2, pred[2]{0:T(512)(128)(4,1)S(1)} %broadcast_compare_fusion.3, ...), kind=kOutput, calls=%fused_computation.3 | convolution fusion | flops 403046400 | bytes 1974294 | tf_op jit(solution)/shard_map/dot_general | solution.py:15
  104.1 1.0 copy.16
  (18 shorter events, 0.3 us)
Async XLA Ops:
  36.6 17.6 %all-to-all-start.1 = ((f32[4,2,64,2,256]{4,3,2,1,0:T(2,128)}), f32[4,2,64,2,256]{4,3,2,1,0:T(2,128)S(1)}, u32[]{:S(2)}, u32[]{:S(2)}) async-start(f32[4,2,64,2,256]{4,3,2,1,0:T(2,128)} %broadcast_in_dim.53), calls=%async_computation.1 | async-start | bytes 2097152 | tf_op jit(solution)/shard_map/all_to_all | solution.py:101
  54.4 7.5 %collective-permute-start = (f32[640,256]{1,0:T(8,128)S(1)}, f32[640,256]{1,0:T(8,128)}, u32[]{:S(2)}, u32[]{:S(2)}) collective-permute-start(f32[640,256]{1,0:T(8,128)S(1)} %pad_maximum_fusion.1), channel_id=1, source_target_pairs={{0,1},{1,0},{8,9},{9,8},{16,17},{17,16},{24,25},{25,24},{32,33},{3... | collective-permute-start | bytes 1966088 | tf_op jit(solution)/shard_map/ppermute | solution.py:127
  85.3 2.5 %copy-start = (f32[512,512]{1,0:T(8,128)S(1)}, f32[512,512]{1,0:T(8,128)}, u32[]{:S(2)}) copy-start(f32[512,512]{1,0:T(8,128)} %factor.1) | copy-start | bytes 3145732
  88.8 3.2 %collective-permute-start.1 = (f32[128,256]{1,0:T(8,128)S(1)}, f32[128,256]{1,0:T(8,128)S(1)}, u32[]{:S(2)}, u32[]{:S(2)}) collective-permute-start(f32[128,256]{1,0:T(8,128)S(1)} %constant_dynamic-slice_fusion), channel_id=1, source_target_pairs={{0,4},{1,5},{8,12},{9,13},{16,20},{17,21},{24,28},{25,29},{32,36},... | collective-permute-start | bytes 393224 | tf_op jit(solution)/shard_map/ppermute | solution.py:137
  92.0 4.2 %collective-permute-start.2 = (f32[128,256]{1,0:T(8,128)S(1)}, f32[128,256]{1,0:T(8,128)S(1)}, u32[]{:S(2)}, u32[]{:S(2)}) collective-permute-start(f32[128,256]{1,0:T(8,128)S(1)} %broadcast_select_fusion.2), channel_id=1, source_target_pairs={{0,2},{1,3},{4,6},{5,7},{8,10},{9,11},{12,14},{13,15},{16,18},{17,... | collective-permute-start | bytes 393224 | tf_op jit(solution)/shard_map/ppermute | solution.py:139
  96.2 6.7 %collective-permute-start.3 = (f32[128,256]{1,0:T(8,128)S(1)}, f32[128,256]{1,0:T(8,128)S(1)}, u32[]{:S(2)}, u32[]{:S(2)}) collective-permute-start(f32[128,256]{1,0:T(8,128)S(1)} %broadcast_select_fusion.3), channel_id=1, source_target_pairs={{0,1},{1,0},{2,3},{3,2},{4,5},{5,4},{6,7},{7,6},{8,9},{9,8},{10,11... | collective-permute-start | bytes 393224 | tf_op jit(solution)/shard_map/ppermute | solution.py:141

commit v2 on v1

v2 whole, which is shorter than its diff:
```python
import functools
import jax
import jax.numpy as jnp
from jax import lax
from jax.experimental import pallas as pl
from jax.experimental.pallas import tpu as pltpu
from jax.sharding import PartitionSpec as P

PANELS = 2
BLOCK = 128
STRIP = 64
HIGHEST = lax.Precision.HIGHEST


def product(left, right, dims=((1,), (0,))):
    return lax.dot_general(left, right, (dims, ((), ())), precision=HIGHEST, preferred_element_type=jnp.float32)

def spread_lane(part, lane, sublane):
    return jnp.where(sublane < 8, jnp.broadcast_to(part[:, lane : lane + 1], (8, 128)), 0.0)


def eliminate(groups, first_lane, work):
    count = len(groups)
    sublane = lax.broadcasted_iota(jnp.int32, (8, 128), 0)
    lane_id = lax.broadcasted_iota(jnp.int32, (8, 128), 1)
    parts = list(groups)
    def spread(i, lane, guard):
        if guard:
            return [spread_lane(parts[i], lane + s, sublane) for s in range(8)]
        return [jnp.broadcast_to(parts[i][:, lane + s : lane + s + 1], (8, 128)) for s in range(8)]
    current = spread(0, first_lane, True)
    for g in range(count):
        lane = first_lane + 8 * g
        more = g + 1 < count
        heads = [current + (spread(g, lane + 8, True) if more else [])]
        if more:
            heads.append(spread(g + 1, lane, False) + spread(g + 1, lane + 8, True))
        for i in range(g + 2, count):
            heads.append(spread(i, lane, False))
        inside = (lane_id >= lane) & (lane_id < lane + 8)
        unit = (lane_id - lane == sublane).astype(jnp.float32)
        for i in range(g, count):
            parts[i] = jnp.where(inside, unit if i == g else 0.0, parts[i])
        scale = None
        for s in range(8):
            below = jnp.where(sublane > s, heads[0][s], 0.0)
            head_rows = [
                jnp.broadcast_to(head[s : s + 1, :], (8, 128)) for head in heads[0][s + 1 :]
            ]
            root = lax.rsqrt(jnp.broadcast_to(heads[0][s][s : s + 1, :], (8, 128)))
            inverse = root * root
            scale = root if s == 0 else jnp.where(sublane == s, root, scale)
            row = jnp.broadcast_to(parts[g][s : s + 1, :], (8, 128))
            if s < 7:
                heads[0][s + 1] = heads[0][s + 1] - (below * head_rows[0]) * inverse
            for i in range(g, count):
                if i == g and s == 7:
                    continue
                factor = (below if i == g else heads[i - g][s]) * inverse
                parts[i] = parts[i] - factor * row
                for p in range(s + 1, len(heads[i - g])):
                    if i > g or p > s + 1:
                        heads[i - g][p] = heads[i - g][p] - factor * head_rows[p - s - 1]
        parts[g] = parts[g] * scale
        if more:
            current = heads[1][8:]
        work()
    return jnp.concatenate(parts, axis=0)


def factor_kernel(first_ref, mine_ref, other_ref, v_ref, x_ref, w_ref, p_ref, e_ref, block_ref):
    size = w_ref.shape[0]
    half = size // 2
    count = size // BLOCK
    first = first_ref[0] == 1
    def left(rows):
        return jnp.where(first, mine_ref[rows, :], other_ref[rows, :])
    def right(rows):
        return jnp.where(first, other_ref[rows, :], mine_ref[rows, :])
    w_ref[:half, :half] = left(slice(0, half))
    w_ref[:, half:] = right(slice(0, size))
    p_ref[:half, :] = left(slice(size, None)).T
    p_ref[half:, :] = right(slice(size, None)).T
    row_id = lax.broadcasted_iota(jnp.int32, (BLOCK, BLOCK), 0)
    col_id = lax.broadcasted_iota(jnp.int32, (BLOCK, BLOCK), 1)
    at = [slice(k * BLOCK, (k + 1) * BLOCK) for k in range(count)]
    pending = []
    for k in range(count):
        slots = 2 * STRIP // 8
        done_slots = [0]
        per = -(-len(pending) // (slots - 2)) if pending else 0
        def work():
            done_slots[0] += 1
            for _ in range(per):
                if pending:
                    pending.pop(0)()
        block_ref[...] = w_ref[at[k], at[k]]
        for begin in range(0, BLOCK, STRIP):
            end = begin + STRIP
            groups = [block_ref[begin + 8 * i : begin + 8 * i + 8, :] for i in range(STRIP // 8)]
            done = eliminate(groups, begin, work)
            rows, lanes = row_id[begin:end], col_id[begin:end]
            block_ref[begin:end, :] = jnp.where(lanes <= rows, done, 0.0)
            if end < BLOCK:
                done = jnp.where((lanes <= rows) | (lanes >= end), done, 0.0)
                rest = block_ref[end:, :]
                rest = jnp.where((col_id[end:] >= begin) & (col_id[end:] < end), 0.0, rest)
                block_ref[end:, :] = rest - product(done.T[end:], done)
        while pending:
            pending.pop(0)()
        e_ref[at[k], at[k]] = block_ref[...]
        if k < count - 1:
            inverse = block_ref[...]
            upper = product(inverse, w_ref[at[k], at[k + 1]])
            w_ref[at[k], at[k + 1]] = upper
            w_ref[at[k + 1], at[k + 1]] -= product(upper.T, upper)
            def panel(k=k, j=0):
                w_ref[at[k], at[j]] = product(e_ref[at[k], at[k]], w_ref[at[k], at[j]])
            def panel_p(k=k):
                p_ref[at[k], :] = product(e_ref[at[k], at[k]], p_ref[at[k], :])
            def panel_e(k=k):
                e_ref[at[k], : k * BLOCK] = product(e_ref[at[k], at[k]], e_ref[at[k], : k * BLOCK])
            def trail(k=k, i=0, j=0):
                w_ref[at[i], at[j]] -= product(w_ref[at[k], at[i]].T, w_ref[at[k], at[j]])
            def trail_p(k=k, i=0):
                p_ref[at[i], :] -= product(w_ref[at[k], at[i]].T, p_ref[at[k], :])
            def trail_e(k=k, i=0):
                lower = w_ref[at[k], at[i]].T
                e_ref[at[i], at[k]] = -product(lower, e_ref[at[k], at[k]])
                if k > 0:
                    e_ref[at[i], : k * BLOCK] -= product(lower, e_ref[at[k], : k * BLOCK])
            def output(k=k):
                solved = p_ref[at[k], :].T
                v_ref[:, at[k]] = solved
                x_ref[:, at[k]] = product(solved, e_ref[at[k], at[k]])
                if k > 0:
                    x_ref[:, : k * BLOCK] += product(solved, e_ref[at[k], : k * BLOCK])
            bind = functools.partial
            for j in range(k + 2, count):
                pending.append(bind(panel, j=j))
            pending.append(bind(panel_p))
            for i in range(k + 1, count):
                for j in range(i, count):
                    if j > k + 1:
                        pending.append(bind(trail, i=i, j=j))
                pending.append(bind(trail_p, i=i))
            if k > 0:
                pending.append(bind(panel_e))
            for i in range(k + 1, count):
                pending.append(bind(trail_e, i=i))
            pending.append(bind(output))
    last = at[count - 1]
    inverse = block_ref[...]
    solved = product(p_ref[last, :], inverse, ((0,), (1,)))
    v_ref[:, last] = solved
    weights = product(solved, inverse)
    x_ref[:, last] = weights
    x_ref[:, : size - BLOCK] += product(weights, e_ref[last, : size - BLOCK])

def weigh(first, mine, other):
    size = 2 * mine.shape[1]
    share = mine.shape[0] - size
    shape = jax.ShapeDtypeStruct((share, size), jnp.float32)
    whole = pl.BlockSpec(memory_space=pltpu.VMEM)
    return pl.pallas_call(
        factor_kernel,
        out_shape=[shape, shape],
        in_specs=[pl.BlockSpec(memory_space=pltpu.SMEM), whole, whole],
        out_specs=[whole, whole],
        scratch_shapes=[
            pltpu.VMEM((size, size), jnp.float32),
            pltpu.VMEM((size, share), jnp.float32),
            pltpu.VMEM((size, size), jnp.float32),
            pltpu.VMEM((BLOCK, BLOCK), jnp.float32),
        ],
        name="factor",
    )(first, mine, other)


def to_all(piece, axis, peers, groups=None):
    copies = jnp.broadcast_to(piece[None], (peers, *piece.shape))
    return lax.all_to_all(copies, axis, 0, 0, axis_index_groups=groups)


def local(schur_window):
    row_blocks, _, width, col_blocks, _, _ = schur_window.shape
    held = schur_window.reshape(row_blocks, width, col_blocks, width)
    layers = lax.axis_size("layer")
    grid_rows = lax.axis_size("row")
    grid_cols = lax.axis_size("col")
    layer_here = lax.axis_index("layer")
    row_here = lax.axis_index("row")
    col_here = lax.axis_index("col")
    x_size = layers // 2
    x_groups = [[x * 2 + z for x in range(x_size)] for z in range(2)]
    share = width // layers
    quarter = width // x_size
    lead = PANELS * width

    head = lax.dynamic_slice(
        schur_window,
        (0, 0, (layer_here // 2) * quarter, 0, 0, 0),
        (1, 1, quarter, col_blocks, 1, width),
    ).reshape(quarter, col_blocks, width)
    quarters = to_all(head, "row", grid_rows)[:PANELS]
    gathered = to_all(quarters, "layer", x_size, x_groups)
    top = jnp.moveaxis(gathered, 0, 1).reshape(lead, col_blocks, width)

    mine = lax.dynamic_slice_in_dim(held, layer_here * share, share, 1)
    mine_first = mine[:, :, 0, :].reshape(row_blocks * share, width)
    swapped_in = jnp.concatenate([top[:, 0, :], mine_first], axis=0)
    swapped = lax.ppermute(swapped_in, "col", [(0, 1), (1, 0)])
    is_first = col_here == 0
    solved, weights = weigh(is_first.astype(jnp.int32)[None], swapped_in, swapped)

    half = lax.dynamic_slice_in_dim(weights, (col_here % 2) * width, width, 1)
    far = lax.ppermute(half, "col", [(0, 4), (1, 5)])
    half = jnp.where(col_here < 4, half, far)
    near = lax.ppermute(half, "col", [(0, 2), (1, 3), (4, 6), (5, 7)])
    half = jnp.where(col_here % 4 < 2, half, near)
    other = lax.ppermute(half, "col", [(i, i ^ 1) for i in range(grid_cols)])
    is_even = col_here % 2 == 0
    weights_here = jnp.concatenate(
        [jnp.where(is_even, half, other), jnp.where(is_even, other, half)], axis=1
    )
    update = product(weights_here, top.reshape(lead, col_blocks * width))
    trailing = mine - update.reshape(row_blocks, share, col_blocks, width)

    row_number = (jnp.arange(row_blocks, dtype=jnp.int32) * grid_rows + row_here)[:, None, None, None]
    col_number = (jnp.arange(col_blocks, dtype=jnp.int32) * grid_cols + col_here)[None, None, :, None]
    row_inside = (jnp.arange(share, dtype=jnp.int32) + layer_here * share)[None, :, None, None]
    col_inside = jnp.arange(width, dtype=jnp.int32)[None, None, None, :]
    panel = jnp.where(is_first, solved[:, :width], solved[:, width : 2 * width])
    panel = panel.reshape(row_blocks, share, 1, width)
    below = (row_number > col_number) | ((row_number == col_number) & (row_inside >= col_inside))
    panel = jnp.where(below, panel, 0.0)
    trailing = jnp.where(row_number < PANELS, 0.0, trailing)
    result = jnp.where(col_number < PANELS, panel, trailing)
    return result.reshape(row_blocks, 1, share, col_blocks, 1, width)


def solution(mesh):
    return jax.shard_map(
        local,
        mesh=mesh,
        in_specs=(P(None, "row", None, None, "col", None),),
        out_specs=P(None, "row", "layer", None, "col", None),
        check_vma=False,
    )
```

time: 106 us -> 98.3 us (0.927)
  Pallas kernels: 21.1 us -> 14.7 us
  matrix products: 4.56 us -> 1.85 us
  local copies, waits for them, and re-layouts: 6.08 us -> 8.38 us
  waiting for transfers between devices: 17.7 us -> 15.9 us
  other arithmetic: 2.61 us -> 4.13 us
    pallas_call x1, Pallas kernels: 21.1 us -> 14.7 us  [weigh(): pl.pallas_call(factor_kernel, out_shape=[shape, shape], in_specs=[pl.Bloc...]
    dot_general x3 -> x1, matrix products: 4.56 us -> 1.85 us  [product(): lax.dot_general(left, right, (dims, ((), ())), precision=HIGHEST, preferr...]
    unnamed x4, local copies, waits for them, and re-layouts: 0.08 us -> 2.63 us
    ppermute x1, waiting for transfers between devices: 2.04 us -> 0.01 us  [local(): near = lax.ppermute(half, 'col', [(0, 2), (1, 3), (4, 6), (5, 7)])]
    slice x1 -> x0, local copies, waits for them, and re-layouts: 1.4 us -> none  [local(): held[0]]
    dot_general x1, local copies, waits for them, and re-layouts: 0.33 us -> 1.55 us  [product(): lax.dot_general(left, right, (dims, ((), ())), precision=HIGHEST, preferr...]
    select_n x1 -> x0, other arithmetic: 1.17 us -> none  [local(): jnp.where(is_first, swapped_in, swapped)]
    concatenate x1 -> x0, other arithmetic: 1.12 us -> none  [local(): jnp.concatenate([jnp.where(is_first, swapped_in, swapped), jnp.where(is_f...]
  transfers between devices with their start and end apart: 5 -> 5, of which waited for: 5 -> 3; matrix products, arithmetic and copies ran while one was open for 2% -> 5% of each run, Pallas kernels for 0% -> 0%
where the time goes in v2:
time: 98.3 us; the launch traced here: 97.8 us
  blocking collectives  33.5 us (34%)
  starting transfers between devices  19.1 us (19%)
  waiting for transfers between devices  15.9 us (16%)
  Pallas kernels  14.7 us (15%)
  local copies, waits for them, and re-layouts  8.38 us (9%)
  other arithmetic  4.13 us (4%)
  matrix products  1.85 us (2%)
    all_to_all x1, blocking collectives, to_all(): return lax.all_to_all(copies, axis, 0, 0, axis_index_groups=groups)  33.5 us
    pallas_call x1, Pallas kernels, weigh(): pl.pallas_call(factor_kernel, out_shape=[shape, shape], in_specs=[pl.Bloc...  14.7 us
    all_to_all x1, waiting for transfers between devices, to_all(): return lax.all_to_all(copies, axis, 0, 0, axis_index_groups=groups)  12.1 us
    ppermute x1, starting transfers between devices, local(): swapped = lax.ppermute(swapped_in, 'col', [(0, 1), (1, 0)])  5.66 us
    all_to_all x1, starting transfers between devices, to_all(): return lax.all_to_all(copies, axis, 0, 0, axis_index_groups=groups)  5.28 us
    ppermute x1, starting transfers between devices, local(): other = lax.ppermute(half, 'col', [(i, i ^ 1) for i in range(grid_cols)])  4.94 us
    unnamed x4, local copies, waits for them, and re-layouts  2.63 us
  transfers between devices with their start and end apart: 5, of which 3 were waited for; matrix products, arithmetic and copies ran while one was open for 5% of the time, Pallas kernels for 0%

profile of v2, /device:TPU:1, one launch (start us, length us, event | category | flops | bytes accessed | tf_op | source)
XLA Modules:
  0.0 97.8 jit_solution(13431189510707439250)
XLA Ops:
  0.0 0.0 copy-start
  0.0 1.6 %copy-done = f32[4,1,256,2,1,256]{5,4,3,2,1,0:T(1,128)S(1)} copy-done((f32[4,1,256,2,1,256]{5,4,3,2,1,0:T(1,128)S(1)}, f32[4,1,256,2,1,256]{5,4,3,2,1,0:T(1,128)}, u32[]{:S(2)}) %copy-start) | copy-done | bytes 2097176
  1.6 0.1 copy.11
  1.7 0.3 broadcast_in_dim.58
  2.0 33.5 %all_to_all.10 = f32[8,64,2,256]{3,2,1,0:T(2,128)S(1)} all-to-all(f32[8,64,2,256]{3,2,1,0:T(2,128)S(1)} %broadcast_in_dim.58), channel_id=1, replica_groups=mesh['layer'=8,'row'=8,'col'=8] {'row'}, dimensions={0} | all-to-all | bytes 2097152 | tf_op jit(solution)/shard_map/all_to_all | solution.py:182
  35.6 1.2 %broadcast_in_dim.59 = f32[4,2,64,2,256]{4,3,2,1,0:T(2,128)} broadcast(f32[2,64,2,256]{3,2,1,0:T(2,128)S(1)} %slice.20), dimensions={1,2,3,4} | broadcast | bytes 1310720 | tf_op jit(solution)/shard_map/broadcast_in_dim | solution.py:181
  36.8 5.3 %all-to-all-start.1 = ((f32[4,2,64,2,256]{4,3,2,1,0:T(2,128)}), f32[4,2,64,2,256]{4,3,2,1,0:T(2,128)S(1)}, u32[]{:S(2)}, u32[]{:S(2)}) async-start(f32[4,2,64,2,256]{4,3,2,1,0:T(2,128)} %broadcast_in_dim.59), calls=%async_computation.1 | async-start | bytes 2097152 | tf_op jit(solution)/shard_map/all_to_all | solution.py:182
  42.1 0.1 constant_dynamic-slice_fusion.1
  42.3 12.1 %all-to-all-done.1 = f32[4,2,64,2,256]{4,3,2,1,0:T(2,128)S(1)} async-done(((f32[4,2,64,2,256]{4,3,2,1,0:T(2,128)}), f32[4,2,64,2,256]{4,3,2,1,0:T(2,128)S(1)}, u32[]{:S(2)}, u32[]{:S(2)}) %all-to-all-start.1) | async-done | bytes 1048608 | tf_op jit(solution)/shard_map/all_to_all | solution.py:182
  54.4 0.1 copy.12
  54.5 0.9 pad_maximum_fusion.mine_ref
  55.4 5.7 %collective-permute-start = (f32[640,256]{1,0:T(8,128)}, f32[640,256]{1,0:T(8,128)}, u32[]{:S(2)}, u32[]{:S(2)}) collective-permute-start(f32[640,256]{1,0:T(8,128)} %pad_maximum_fusion.mine_ref), channel_id=1, source_target_pairs={{0,1},{1,0},{8,9},{9,8},{16,17},{17,16},{24,25},{25,24},{32,33},{3... | collective-permute-start | bytes 1966088 | tf_op jit(solution)/shard_map/ppermute | solution.py:212
  61.1 0.1 iota_compare_fusion
  61.2 1.9 %collective-permute-done.other_ref = f32[640,256]{1,0:T(8,128)} collective-permute-done((f32[640,256]{1,0:T(8,128)}, f32[640,256]{1,0:T(8,128)}, u32[]{:S(2)}, u32[]{:S(2)}) %collective-permute-start) | collective-permute-done | bytes 655392 | tf_op jit(solution)/shard_map/ppermute | solution.py:212
  63.1 14.7 %factor.1 = (f32[128,512]{1,0:T(8,128)}, f32[128,512]{1,0:T(8,128)}) custom-call(s32[1]{0:T(128)} %bitcast.first_ref, f32[640,256]{1,0:T(8,128)} %pad_maximum_fusion.mine_ref, f32[640,256]{1,0:T(8,128)} %collective-permute-done.other_ref), custom_call_target="tpu_custom_call" | custom-call | tf_op jit(solution)/shard_map/factor/pallas_call | solution.py:165
  77.9 0.9 constant_dynamic-slice_fusion
  78.8 1.3 %collective-permute-start.1 = (f32[128,256]{1,0:T(8,128)S(1)}, f32[128,256]{1,0:T(8,128)S(1)}, u32[]{:S(2)}, u32[]{:S(2)}) collective-permute-start(f32[128,256]{1,0:T(8,128)S(1)} %constant_dynamic-slice_fusion), channel_id=1, source_target_pairs={{0,4},{1,5},{8,12},{9,13},{16,20},{17,21},{24,28},{25,29},{32,36},... | collective-permute-start | bytes 393224 | tf_op jit(solution)/shard_map/ppermute | solution.py:217
  80.1 0.1 broadcast_compare_fusion.1
  80.2 1.8 %collective-permute-done.1 = f32[128,256]{1,0:T(8,128)S(1)} collective-permute-done((f32[128,256]{1,0:T(8,128)S(1)}, f32[128,256]{1,0:T(8,128)S(1)}, u32[]{:S(2)}, u32[]{:S(2)}) %collective-permute-start.1) | collective-permute-done | bytes 131104 | tf_op jit(solution)/shard_map/ppermute | solution.py:217
  82.0 0.9 broadcast_select_fusion
  82.9 2.0 %collective-permute-start.2 = (f32[128,256]{1,0:T(8,128)S(1)}, f32[128,256]{1,0:T(8,128)}, u32[]{:S(2)}, u32[]{:S(2)}) collective-permute-start(f32[128,256]{1,0:T(8,128)S(1)} %broadcast_select_fusion), channel_id=1, source_target_pairs={{0,2},{1,3},{4,6},{5,7},{8,10},{9,11},{12,14},{13,15},{16,18},{17,... | collective-permute-start | bytes 393224 | tf_op jit(solution)/shard_map/ppermute | solution.py:219
  84.9 0.5 broadcast_compare_fusion.3
  85.4 0.6 broadcast_compare_fusion.2
  86.0 0.4 copy.14
  86.4 1.0 %copy.19 = f32[64,8,2,256]{3,1,2,0:T(8,128)} copy(f32[64,8,2,256]{3,2,1,0:T(2,128)S(1)} %bitcast.35) | data formatting | bytes 2097152
  87.4 1.6 %copy.15 = f32[512,512]{1,0:T(8,128)S(1)} copy(f32[512,512]{0,1:T(8,128)} %bitcast.36) | data formatting | bytes 2097152 | tf_op jit(solution)/shard_map/dot_general | solution.py:16
  88.9 0.0 collective-permute-done.2
  89.0 4.9 %collective-permute-start.3 = (f32[128,256]{1,0:T(8,128)S(1)}, f32[128,256]{1,0:T(8,128)S(1)}, u32[]{:S(2)}, u32[]{:S(2)}) collective-permute-start(f32[128,256]{1,0:T(8,128)S(1)} %broadcast_select_fusion.1), channel_id=1, source_target_pairs={{0,1},{1,0},{2,3},{3,2},{4,5},{5,4},{6,7},{7,6},{8,9},{9,8},{10,11... | collective-permute-start | bytes 393224 | tf_op jit(solution)/shard_map/ppermute | solution.py:221
  93.9 1.0 %slice_select_fusion = f32[128,256]{1,0:T(8,128)S(1)} fusion(f32[128,512]{1,0:T(8,128)} %get-tuple-element.7, pred[]{:T(512)S(6)} %eq.25), kind=kLoop, calls=%fused_computation.9 | loop fusion | flops 32768 | bytes 393217 | tf_op jit(solution)/shard_map/jit(_where)/select_n | solution.py:233
  94.9 0.0 collective-permute-done.3
  95.0 1.9 %fusion.2 = f32[4,1,32,2,1,256]{5,2,3,0,4,1:T(8,128)S(1)} fusion(f32[4,32,512,1]{2,1,3,0:T(8,128)S(1)} %bitcast.38, f32[2,256,512,1]{2,1,0,3:T(8,128)S(1)} %bitcast.34, f32[4,32,256]{2,1,0:T(8,128)S(1)} %bitcast.40, pred[4]{0:T(512)(128)(4,1)} %broadcast_compare_fusion.2, pred[2]{0:T(512)(128)(4,1)} %broadcast_compare_fusion.3, ...), kind=kOutput, calls=%fused_computation.3 | convolution fusion | flops 403046400 | bytes 1974294 | tf_op jit(solution)/shard_map/dot_general | solution.py:16
  96.9 1.0 copy.16
  (12 shorter events, 0.2 us)
Async XLA Ops:
  0.0 1.6 %copy-start = (f32[4,1,256,2,1,256]{5,4,3,2,1,0:T(1,128)S(1)}, f32[4,1,256,2,1,256]{5,4,3,2,1,0:T(1,128)}, u32[]{:S(2)}) copy-start(f32[4,1,256,2,1,256]{5,4,3,2,1,0:T(1,128)} %param.1) | copy-start | bytes 6291460
  36.8 17.6 %all-to-all-start.1 = ((f32[4,2,64,2,256]{4,3,2,1,0:T(2,128)}), f32[4,2,64,2,256]{4,3,2,1,0:T(2,128)S(1)}, u32[]{:S(2)}, u32[]{:S(2)}) async-start(f32[4,2,64,2,256]{4,3,2,1,0:T(2,128)} %broadcast_in_dim.59), calls=%async_computation.1 | async-start | bytes 2097152 | tf_op jit(solution)/shard_map/all_to_all | solution.py:182
  55.4 7.7 %collective-permute-start = (f32[640,256]{1,0:T(8,128)}, f32[640,256]{1,0:T(8,128)}, u32[]{:S(2)}, u32[]{:S(2)}) collective-permute-start(f32[640,256]{1,0:T(8,128)} %pad_maximum_fusion.mine_ref), channel_id=1, source_target_pairs={{0,1},{1,0},{8,9},{9,8},{16,17},{17,16},{24,25},{25,24},{32,33},{3... | collective-permute-start | bytes 1966088 | tf_op jit(solution)/shard_map/ppermute | solution.py:212
  78.8 3.2 %collective-permute-start.1 = (f32[128,256]{1,0:T(8,128)S(1)}, f32[128,256]{1,0:T(8,128)S(1)}, u32[]{:S(2)}, u32[]{:S(2)}) collective-permute-start(f32[128,256]{1,0:T(8,128)S(1)} %constant_dynamic-slice_fusion), channel_id=1, source_target_pairs={{0,4},{1,5},{8,12},{9,13},{16,20},{17,21},{24,28},{25,29},{32,36},... | collective-permute-start | bytes 393224 | tf_op jit(solution)/shard_map/ppermute | solution.py:217
  82.9 6.0 %collective-permute-start.2 = (f32[128,256]{1,0:T(8,128)S(1)}, f32[128,256]{1,0:T(8,128)}, u32[]{:S(2)}, u32[]{:S(2)}) collective-permute-start(f32[128,256]{1,0:T(8,128)S(1)} %broadcast_select_fusion), channel_id=1, source_target_pairs={{0,2},{1,3},{4,6},{5,7},{8,10},{9,11},{12,14},{13,15},{16,18},{17,... | collective-permute-start | bytes 393224 | tf_op jit(solution)/shard_map/ppermute | solution.py:219
  89.0 5.9 %collective-permute-start.3 = (f32[128,256]{1,0:T(8,128)S(1)}, f32[128,256]{1,0:T(8,128)S(1)}, u32[]{:S(2)}, u32[]{:S(2)}) collective-permute-start(f32[128,256]{1,0:T(8,128)S(1)} %broadcast_select_fusion.1), channel_id=1, source_target_pairs={{0,1},{1,0},{2,3},{3,2},{4,5},{5,4},{6,7},{7,6},{8,9},{9,8},{10,11... | collective-permute-start | bytes 393224 | tf_op jit(solution)/shard_map/ppermute | solution.py:221

commit v3 on v2

--- a/solution.py
+++ b/solution.py
@@ -68,7 +68,9 @@
     return jnp.concatenate(parts, axis=0)
 
 
-def factor_kernel(first_ref, mine_ref, other_ref, v_ref, x_ref, w_ref, p_ref, e_ref, block_ref):
+def factor_kernel(
+    first_ref, mine_ref, other_ref, panel_ref, half_ref, v_ref, x_ref, w_ref, p_ref, e_ref, block_ref
+):
     size = w_ref.shape[0]
     half = size // 2
     count = size // BLOCK
@@ -156,11 +158,13 @@
     weights = product(solved, inverse)
     x_ref[:, last] = weights
     x_ref[:, : size - BLOCK] += product(weights, e_ref[last, : size - BLOCK])
+    panel_ref[...] = jnp.where(first, v_ref[:, :half], v_ref[:, half:])
+    half_ref[...] = jnp.where(first, x_ref[:, :half], x_ref[:, half:])
 
 def weigh(first, mine, other):
     size = 2 * mine.shape[1]
     share = mine.shape[0] - size
-    shape = jax.ShapeDtypeStruct((share, size), jnp.float32)
+    shape = jax.ShapeDtypeStruct((share, size // 2), jnp.float32)
     whole = pl.BlockSpec(memory_space=pltpu.VMEM)
     return pl.pallas_call(
         factor_kernel,
@@ -168,6 +172,8 @@
         in_specs=[pl.BlockSpec(memory_space=pltpu.SMEM), whole, whole],
         out_specs=[whole, whole],
         scratch_shapes=[
+            pltpu.VMEM((share, size), jnp.float32),
+            pltpu.VMEM((share, size), jnp.float32),
             pltpu.VMEM((size, size), jnp.float32),
             pltpu.VMEM((size, share), jnp.float32),
             pltpu.VMEM((size, size), jnp.float32),
@@ -202,18 +208,22 @@
         (0, 0, (layer_here // 2) * quarter, 0, 0, 0),
         (1, 1, quarter, col_blocks, 1, width),
     ).reshape(quarter, col_blocks, width)
-    quarters = to_all(head, "row", grid_rows)[:PANELS]
-    gathered = to_all(quarters, "layer", x_size, x_groups)
-    top = jnp.moveaxis(gathered, 0, 1).reshape(lead, col_blocks, width)
-
+    def collect(part, name):
+        with jax.named_scope(name + "_row"):
+            quarters = to_all(part, "row", grid_rows)[:PANELS]
+        with jax.named_scope(name + "_x"):
+            gathered = to_all(quarters, "layer", x_size, x_groups)
+        return jnp.moveaxis(gathered, 0, 1).reshape(lead, -1)
+
+    lead_part = collect(head[:, 0, :], "lead")
+    rest_part = collect(head[:, 1:, :].reshape(quarter, (col_blocks - 1) * width), "rest")
     mine = lax.dynamic_slice_in_dim(held, layer_here * share, share, 1)
     mine_first = mine[:, :, 0, :].reshape(row_blocks * share, width)
-    swapped_in = jnp.concatenate([top[:, 0, :], mine_first], axis=0)
+    swapped_in = jnp.concatenate([lead_part, mine_first], axis=0)
     swapped = lax.ppermute(swapped_in, "col", [(0, 1), (1, 0)])
     is_first = col_here == 0
-    solved, weights = weigh(is_first.astype(jnp.int32)[None], swapped_in, swapped)
-
-    half = lax.dynamic_slice_in_dim(weights, (col_here % 2) * width, width, 1)
+    with jax.named_scope("inverse"):
+        panel, half = weigh(is_first.astype(jnp.int32)[None], swapped_in, swapped)
     far = lax.ppermute(half, "col", [(0, 4), (1, 5)])
     half = jnp.where(col_here < 4, half, far)
     near = lax.ppermute(half, "col", [(0, 2), (1, 3), (4, 6), (5, 7)])
@@ -223,14 +233,13 @@
     weights_here = jnp.concatenate(
         [jnp.where(is_even, half, other), jnp.where(is_even, other, half)], axis=1
     )
-    update = product(weights_here, top.reshape(lead, col_blocks * width))
+    update = product(weights_here, jnp.concatenate([lead_part, rest_part], axis=1))
     trailing = mine - update.reshape(row_blocks, share, col_blocks, width)
 
     row_number = (jnp.arange(row_blocks, dtype=jnp.int32) * grid_rows + row_here)[:, None, None, None]
     col_number = (jnp.arange(col_blocks, dtype=jnp.int32) * grid_cols + col_here)[None, None, :, None]
     row_inside = (jnp.arange(share, dtype=jnp.int32) + layer_here * share)[None, :, None, None]
     col_inside = jnp.arange(width, dtype=jnp.int32)[None, None, None, :]
-    panel = jnp.where(is_first, solved[:, :width], solved[:, width : 2 * width])
     panel = panel.reshape(row_blocks, share, 1, width)
     below = (row_number > col_number) | ((row_number == col_number) & (row_inside >= col_inside))
     panel = jnp.where(below, panel, 0.0)

time: 98.3 us -> 93.6 us (0.952)
  the two profiles are of different devices: /device:TPU:1 before, /device:TPU:8 now
where the time goes in v3:
time: 93.6 us; the launch traced here: 93 us
  starting transfers between devices  24.7 us (26%)
  blocking collectives  23.4 us (25%)
  waiting for transfers between devices  15.3 us (16%)
  Pallas kernels  14.7 us (16%)
  local copies, waits for them, and re-layouts  8.8 us (9%)
  other arithmetic  5.2 us (6%)
    all_to_all x1, blocking collectives, to_all(): return lax.all_to_all(copies, axis, 0, 0, axis_index_groups=groups)  23.4 us
    pallas_call x1, Pallas kernels, weigh(): pl.pallas_call(factor_kernel, out_shape=[shape, shape], in_specs=[pl.Bloc...  14.7 us
    all_to_all x3, starting transfers between devices, to_all(): return lax.all_to_all(copies, axis, 0, 0, axis_index_groups=groups)  13.2 us
    all_to_all x3, waiting for transfers between devices, to_all(): return lax.all_to_all(copies, axis, 0, 0, axis_index_groups=groups)  11.3 us
    ppermute x1, starting transfers between devices, local(): far = lax.ppermute(half, 'col', [(0, 4), (1, 5)])  5.67 us
    ppermute x1, waiting for transfers between devices, local(): far = lax.ppermute(half, 'col', [(0, 4), (1, 5)])  3.91 us
    broadcast_in_dim x4, local copies, waits for them, and re-layouts, to_all(): copies = jnp.broadcast_to(piece[None], (peers, *piece.shape))  2.56 us
    unnamed x16, local copies, waits for them, and re-layouts  2.55 us
  transfers between devices with their start and end apart: 7, of which 3 were waited for; matrix products, arithmetic and copies ran while one was open for 8% of the time, Pallas kernels for 16%

profile of v3, /device:TPU:8, one launch (start us, length us, event | category | flops | bytes accessed | tf_op | source)
XLA Modules:
  0.0 93.0 jit_solution(13613225087627675939)
XLA Ops:
  0.0 0.0 copy-start
  0.0 1.6 %copy-done = f32[4,1,256,2,1,256]{5,4,3,2,1,0:T(1,128)S(1)} copy-done((f32[4,1,256,2,1,256]{5,4,3,2,1,0:T(1,128)S(1)}, f32[4,1,256,2,1,256]{5,4,3,2,1,0:T(1,128)}, u32[]{:S(2)}) %copy-start) | copy-done | bytes 2097176
  1.6 0.1 copy.26
  1.7 0.7 fusion.10
  2.5 23.4 %all_to_all.20 = f32[8,64,256]{2,1,0:T(8,128)S(1)} all-to-all(f32[8,64,256]{2,1,0:T(8,128)S(1)} %broadcast_in_dim.71), channel_id=1, replica_groups=mesh['layer'=8,'row'=8,'col'=8] {'row'}, dimensions={0} | all-to-all | bytes 1048576 | tf_op jit(solution)/shard_map/lead_row/all_to_all | solution.py:188
  25.9 0.8 broadcast_in_dim.72
  26.7 4.3 %all-to-all-start.1 = ((f32[4,2,64,256]{3,2,1,0:T(8,128)}), f32[4,2,64,256]{3,2,1,0:T(8,128)S(1)}, u32[]{:S(2)}, u32[]{:S(2)}) async-start(f32[4,2,64,256]{3,2,1,0:T(8,128)} %broadcast_in_dim.72), calls=%async_computation.1 | async-start | bytes 1048576 | tf_op jit(solution)/shard_map/lead_x/all_to_all | solution.py:188
  31.0 0.1 constant_dynamic-slice_fusion
  31.2 0.7 slice.22
  31.8 7.3 %all-to-all-done.1 = f32[4,2,64,256]{3,2,1,0:T(8,128)S(1)} async-done(((f32[4,2,64,256]{3,2,1,0:T(8,128)}), f32[4,2,64,256]{3,2,1,0:T(8,128)S(1)}, u32[]{:S(2)}, u32[]{:S(2)}) %all-to-all-start.1) | async-done | bytes 524320 | tf_op jit(solution)/shard_map/lead_x/all_to_all | solution.py:188
  39.1 1.0 %pad_maximum_fusion.mine_ref = f32[640,256]{1,0:T(8,128)S(1)} fusion(f32[128,256]{1,0:T(8,128)} %bitcast.25, f32[512,256]{1,0:T(8,128)S(1)} %bitcast.19), kind=kLoop, calls=%fused_computation.4 | loop fusion | flops 163840 | bytes 1310720 | tf_op jit(solution)/shard_map/concatenate | solution.py:222
  40.1 0.0 copy-start.1
  40.1 1.9 %collective-permute-start = (f32[640,256]{1,0:T(8,128)S(1)}, f32[640,256]{1,0:T(8,128)}, u32[]{:S(2)}, u32[]{:S(2)}) collective-permute-start(f32[640,256]{1,0:T(8,128)S(1)} %pad_maximum_fusion.mine_ref), channel_id=1, source_target_pairs={{0,1},{1,0},{8,9},{9,8},{16,17},{17,16},{24,25},{25,24},{32,33},{3... | collective-permute-start | bytes 1966088 | tf_op jit(solution)/shard_map/ppermute | solution.py:223
  42.0 0.8 copy.27
  42.9 0.8 broadcast_in_dim.78
  43.7 5.5 %all-to-all-start.2 = ((f32[8,64,256]{2,1,0:T(8,128)}), f32[8,64,256]{2,1,0:T(8,128)}, u32[]{:S(2)}, u32[]{:S(2)}) async-start(f32[8,64,256]{2,1,0:T(8,128)} %broadcast_in_dim.78), calls=%async_computation.2 | async-start | bytes 1048576 | tf_op jit(solution)/shard_map/rest_row/all_to_all | solution.py:188
  49.2 0.1 iota_compare_fusion
  49.3 0.0 collective-permute-done.other_ref
  49.3 0.0 copy-done.1
  49.3 14.7 %factor.1 = (f32[128,256]{1,0:T(8,128)}, f32[128,256]{1,0:T(8,128)}) custom-call(s32[1]{0:T(128)} %bitcast.first_ref, f32[640,256]{1,0:T(8,128)} %copy-done.1, f32[640,256]{1,0:T(8,128)} %collective-permute-done.other_ref), custom_call_target="tpu_custom_call" | custom-call | tf_op jit(solution)/shard_map/inverse/factor/pallas_call | solution.py:169
  64.0 5.7 %collective-permute-start.1 = (f32[128,256]{1,0:T(8,128)}, f32[128,256]{1,0:T(8,128)S(1)}, u32[]{:S(2)}, u32[]{:S(2)}) collective-permute-start(f32[128,256]{1,0:T(8,128)} %get-tuple-element.8), channel_id=1, source_target_pairs={{0,4},{1,5},{8,12},{9,13},{16,20},{17,21},{24,28},{25,29},{32,36},... | collective-permute-start | bytes 393224 | tf_op jit(solution)/shard_map/ppermute | solution.py:227
  69.7 3.9 %collective-permute-done.1 = f32[128,256]{1,0:T(8,128)S(1)} collective-permute-done((f32[128,256]{1,0:T(8,128)}, f32[128,256]{1,0:T(8,128)S(1)}, u32[]{:S(2)}, u32[]{:S(2)}) %collective-permute-start.1) | collective-permute-done | bytes 131104 | tf_op jit(solution)/shard_map/ppermute | solution.py:227
  73.6 0.9 broadcast_select_fusion
  74.5 0.0 copy-start.2
  74.5 2.0 %collective-permute-start.2 = (f32[128,256]{1,0:T(8,128)S(1)}, f32[128,256]{1,0:T(8,128)}, u32[]{:S(2)}, u32[]{:S(2)}) collective-permute-start(f32[128,256]{1,0:T(8,128)S(1)} %broadcast_select_fusion), channel_id=1, source_target_pairs={{0,2},{1,3},{4,6},{5,7},{8,10},{9,11},{12,14},{13,15},{16,18},{17,... | collective-permute-start | bytes 393224 | tf_op jit(solution)/shard_map/ppermute | solution.py:229
  76.5 0.1 broadcast_compare_fusion.1
  76.6 0.0 all-to-all-done.2
  76.6 0.9 slice.24
  77.5 0.8 broadcast_in_dim.79
  78.3 3.5 %all-to-all-start.3 = ((f32[4,2,64,256]{3,2,1,0:T(8,128)}), f32[4,2,64,256]{3,2,1,0:T(8,128)S(1)}, u32[]{:S(2)}, u32[]{:S(2)}) async-start(f32[4,2,64,256]{3,2,1,0:T(8,128)} %broadcast_in_dim.79), calls=%async_computation.3 | async-start | bytes 1048576 | tf_op jit(solution)/shard_map/rest_x/all_to_all | solution.py:188
  81.8 0.0 copy-done.2
  81.8 0.0 collective-permute-done.2
  81.8 0.9 %broadcast_select_fusion.1 = f32[128,256]{1,0:T(8,128)S(1)} fusion(f32[128,256]{1,0:T(8,128)} %copy-done.2, f32[128,256]{1,0:T(8,128)} %collective-permute-done.2, pred[]{:T(512)S(6)} %lt.44), kind=kLoop, calls=%fused_computation.16 | loop fusion | flops 32768 | bytes 393217 | tf_op jit(solution)/shard_map/jit(_where)/select_n | solution.py:230
  82.8 1.9 %collective-permute-start.3 = (f32[128,256]{1,0:T(8,128)S(1)}, f32[128,256]{1,0:T(8,128)}, u32[]{:S(2)}, u32[]{:S(2)}) collective-permute-start(f32[128,256]{1,0:T(8,128)S(1)} %broadcast_select_fusion.1), channel_id=1, source_target_pairs={{0,1},{1,0},{2,3},{3,2},{4,5},{5,4},{6,7},{7,6},{8,9},{9,8},{10,11... | collective-permute-start | bytes 393224 | tf_op jit(solution)/shard_map/ppermute | solution.py:231
  84.7 0.5 broadcast_compare_fusion.3
  85.2 0.6 broadcast_compare_fusion.2
  85.8 4.1 %all-to-all-done.3 = f32[4,2,64,256]{3,2,1,0:T(8,128)S(1)} async-done(((f32[4,2,64,256]{3,2,1,0:T(8,128)}), f32[4,2,64,256]{3,2,1,0:T(8,128)S(1)}, u32[]{:S(2)}, u32[]{:S(2)}) %all-to-all-start.3) | async-done | bytes 524320 | tf_op jit(solution)/shard_map/rest_x/all_to_all | solution.py:188
  89.9 0.0 copy-start.3
  89.9 0.0 copy-start.4
  89.9 0.0 copy-start.5
  89.9 0.0 collective-permute-done.3
  89.9 1.0 %broadcast_select_fusion.3 = (f32[128,256]{1,0:T(8,128)S(1)}, f32[128,256]{1,0:T(8,128)S(1)}) fusion(f32[128,256]{1,0:T(8,128)S(1)} %broadcast_select_fusion.1, f32[128,256]{1,0:T(8,128)} %collective-permute-done.3, pred[]{:T(512)S(6)} %eq.25), kind=kLoop, calls=%fused_computation.18 | loop fusion | flops 65536 | bytes 524289 | tf_op jit(solution)/shard_map/jit(_where)/select_n | solution.py:234
  90.9 0.7 fusion
  91.6 0.2 reshape.141
  91.8 0.0 copy-done.3
  91.8 0.0 copy-done.4
  91.8 0.0 copy-done.5
  91.8 0.2 fusion.8
  92.0 1.0 %copy.10 = f32[4,1,32,2,1,256]{5,4,3,2,1,0:T(1,128)} copy(f32[4,1,32,2,1,256]{5,2,4,3,1,0:T(8,128)S(1)} %fusion.8) | data formatting | bytes 524288 | tf_op jit(solution)/shard_map/jit(_where)/select_n | solution.py:247
  (10 shorter events, 0.2 us)
Async XLA Ops:
  0.0 1.6 %copy-start = (f32[4,1,256,2,1,256]{5,4,3,2,1,0:T(1,128)S(1)}, f32[4,1,256,2,1,256]{5,4,3,2,1,0:T(1,128)}, u32[]{:S(2)}) copy-start(f32[4,1,256,2,1,256]{5,4,3,2,1,0:T(1,128)} %param.1) | copy-start | bytes 6291460
  26.7 12.4 %all-to-all-start.1 = ((f32[4,2,64,256]{3,2,1,0:T(8,128)}), f32[4,2,64,256]{3,2,1,0:T(8,128)S(1)}, u32[]{:S(2)}, u32[]{:S(2)}) async-start(f32[4,2,64,256]{3,2,1,0:T(8,128)} %broadcast_in_dim.72), calls=%async_computation.1 | async-start | bytes 1048576 | tf_op jit(solution)/shard_map/lead_x/all_to_all | solution.py:188
  40.1 9.2 %copy-start.1 = (f32[640,256]{1,0:T(8,128)}, f32[640,256]{1,0:T(8,128)S(1)}, u32[]{:S(2)}) copy-start(f32[640,256]{1,0:T(8,128)S(1)} %pad_maximum_fusion.mine_ref) | copy-start | bytes 1966084
  40.1 9.2 %collective-permute-start = (f32[640,256]{1,0:T(8,128)S(1)}, f32[640,256]{1,0:T(8,128)}, u32[]{:S(2)}, u32[]{:S(2)}) collective-permute-start(f32[640,256]{1,0:T(8,128)S(1)} %pad_maximum_fusion.mine_ref), channel_id=1, source_target_pairs={{0,1},{1,0},{8,9},{9,8},{16,17},{17,16},{24,25},{25,24},{32,33},{3... | collective-permute-start | bytes 1966088 | tf_op jit(solution)/shard_map/ppermute | solution.py:223
  43.7 32.9 %all-to-all-start.2 = ((f32[8,64,256]{2,1,0:T(8,128)}), f32[8,64,256]{2,1,0:T(8,128)}, u32[]{:S(2)}, u32[]{:S(2)}) async-start(f32[8,64,256]{2,1,0:T(8,128)} %broadcast_in_dim.78), calls=%async_computation.2 | async-start | bytes 1048576 | tf_op jit(solution)/shard_map/rest_row/all_to_all | solution.py:188
  64.0 9.6 %collective-permute-start.1 = (f32[128,256]{1,0:T(8,128)}, f32[128,256]{1,0:T(8,128)S(1)}, u32[]{:S(2)}, u32[]{:S(2)}) collective-permute-start(f32[128,256]{1,0:T(8,128)} %get-tuple-element.8), channel_id=1, source_target_pairs={{0,4},{1,5},{8,12},{9,13},{16,20},{17,21},{24,28},{25,29},{32,36},... | collective-permute-start | bytes 393224 | tf_op jit(solution)/shard_map/ppermute | solution.py:227
  74.5 7.3 %copy-start.2 = (f32[128,256]{1,0:T(8,128)}, f32[128,256]{1,0:T(8,128)S(1)}, u32[]{:S(2)}) copy-start(f32[128,256]{1,0:T(8,128)S(1)} %broadcast_select_fusion) | copy-start | bytes 393220
  74.5 7.3 %collective-permute-start.2 = (f32[128,256]{1,0:T(8,128)S(1)}, f32[128,256]{1,0:T(8,128)}, u32[]{:S(2)}, u32[]{:S(2)}) collective-permute-start(f32[128,256]{1,0:T(8,128)S(1)} %broadcast_select_fusion), channel_id=1, source_target_pairs={{0,2},{1,3},{4,6},{5,7},{8,10},{9,11},{12,14},{13,15},{16,18},{17,... | collective-permute-start | bytes 393224 | tf_op jit(solution)/shard_map/ppermute | solution.py:229
  78.3 11.5 %all-to-all-start.3 = ((f32[4,2,64,256]{3,2,1,0:T(8,128)}), f32[4,2,64,256]{3,2,1,0:T(8,128)S(1)}, u32[]{:S(2)}, u32[]{:S(2)}) async-start(f32[4,2,64,256]{3,2,1,0:T(8,128)} %broadcast_in_dim.79), calls=%async_computation.3 | async-start | bytes 1048576 | tf_op jit(solution)/shard_map/rest_x/all_to_all | solution.py:188
  82.8 7.2 %collective-permute-start.3 = (f32[128,256]{1,0:T(8,128)S(1)}, f32[128,256]{1,0:T(8,128)}, u32[]{:S(2)}, u32[]{:S(2)}) collective-permute-start(f32[128,256]{1,0:T(8,128)S(1)} %broadcast_select_fusion.1), channel_id=1, source_target_pairs={{0,1},{1,0},{2,3},{3,2},{4,5},{5,4},{6,7},{7,6},{8,9},{9,8},{10,11... | collective-permute-start | bytes 393224 | tf_op jit(solution)/shard_map/ppermute | solution.py:231
  89.9 1.9 %copy-start.3 = (f32[128,256]{1,0:T(8,128)S(1)}, f32[128,256]{1,0:T(8,128)}, u32[]{:S(2)}) copy-start(f32[128,256]{1,0:T(8,128)} %get-tuple-element.7) | copy-start | bytes 393220
  89.9 1.9 %copy-start.4 = (pred[2]{0:T(512)(128)(4,1)S(1)}, pred[2]{0:T(512)(128)(4,1)}, u32[]{:S(2)}) copy-start(pred[2]{0:T(512)(128)(4,1)} %broadcast_compare_fusion.3) | copy-start | bytes 10
  89.9 1.9 %copy-start.5 = (pred[4]{0:T(512)(128)(4,1)S(1)}, pred[4]{0:T(512)(128)(4,1)}, u32[]{:S(2)}) copy-start(pred[4]{0:T(512)(128)(4,1)} %broadcast_compare_fusion.2) | copy-start | bytes 16

commit v4 on v3

--- a/solution.py
+++ b/solution.py
@@ -179,6 +179,7 @@
             pltpu.VMEM((size, size), jnp.float32),
             pltpu.VMEM((BLOCK, BLOCK), jnp.float32),
         ],
+        compiler_params=pltpu.CompilerParams(vmem_limit_bytes=16 << 20),
         name="factor",
     )(first, mine, other)
 

time: 93.6 us -> 91.2 us (0.974)
  waiting for transfers between devices: 15.3 us -> 13.7 us
  Pallas kernels: 14.7 us -> 13.4 us
    unnamed x16 -> x18, local copies, waits for them, and re-layouts: 2.55 us -> 4.03 us
    pallas_call x1, Pallas kernels: 14.7 us -> 13.4 us  [weigh(): pl.pallas_call(factor_kernel, out_shape=[shape, shape], in_specs=[pl.Bloc...]
  transfers between devices with their start and end apart: 7 -> 7, of which waited for: 3 -> 3; matrix products, arithmetic and copies ran while one was open for 8% -> 9% of each run, Pallas kernels for 16% -> 15%
where the time goes in v4:
time: 91.2 us; the launch traced here: 90.7 us
  starting transfers between devices  23.9 us (26%)
  blocking collectives  23.4 us (26%)
  waiting for transfers between devices  13.7 us (15%)
  Pallas kernels  13.4 us (15%)
  local copies, waits for them, and re-layouts  9.64 us (11%)
  other arithmetic  5.69 us (6%)
    all_to_all x1, blocking collectives, to_all(): return lax.all_to_all(copies, axis, 0, 0, axis_index_groups=groups)  23.4 us
    pallas_call x1, Pallas kernels, weigh(): pl.pallas_call(factor_kernel, out_shape=[shape, shape], in_specs=[pl.Bloc...  13.4 us
    all_to_all x3, starting transfers between devices, to_all(): return lax.all_to_all(copies, axis, 0, 0, axis_index_groups=groups)  13.2 us
    all_to_all x3, waiting for transfers between devices, to_all(): return lax.all_to_all(copies, axis, 0, 0, axis_index_groups=groups)  10.6 us
    ppermute x1, starting transfers between devices, local(): far = lax.ppermute(half, 'col', [(0, 4), (1, 5)])  4.87 us
    unnamed x18, local copies, waits for them, and re-layouts  4.03 us
    ppermute x1, waiting for transfers between devices, local(): far = lax.ppermute(half, 'col', [(0, 4), (1, 5)])  3.06 us
    broadcast_in_dim x4, local copies, waits for them, and re-layouts, to_all(): copies = jnp.broadcast_to(piece[None], (peers, *piece.shape))  2.57 us
  transfers between devices with their start and end apart: 7, of which 3 were waited for; matrix products, arithmetic and copies ran while one was open for 9% of the time, Pallas kernels for 15%

profile of v4, /device:TPU:8, one launch (start us, length us, event | category | flops | bytes accessed | tf_op | source)
XLA Modules:
  0.0 90.7 jit_solution(16225907399167294565)
XLA Ops:
  0.0 0.0 copy-start
  0.0 1.6 %copy-done = f32[4,1,256,2,1,256]{5,4,3,2,1,0:T(1,128)S(1)} copy-done((f32[4,1,256,2,1,256]{5,4,3,2,1,0:T(1,128)S(1)}, f32[4,1,256,2,1,256]{5,4,3,2,1,0:T(1,128)}, u32[]{:S(2)}) %copy-start) | copy-done | bytes 2097176
  1.6 0.1 copy.26
  1.7 0.7 fusion.10
  2.5 23.4 %all_to_all.20 = f32[8,64,256]{2,1,0:T(8,128)S(1)} all-to-all(f32[8,64,256]{2,1,0:T(8,128)S(1)} %broadcast_in_dim.71), channel_id=1, replica_groups=mesh['layer'=8,'row'=8,'col'=8] {'row'}, dimensions={0} | all-to-all | bytes 1048576 | tf_op jit(solution)/shard_map/lead_row/all_to_all | solution.py:189
  25.9 0.8 broadcast_in_dim.72
  26.7 4.3 %all-to-all-start.1 = ((f32[4,2,64,256]{3,2,1,0:T(8,128)}), f32[4,2,64,256]{3,2,1,0:T(8,128)S(1)}, u32[]{:S(2)}, u32[]{:S(2)}) async-start(f32[4,2,64,256]{3,2,1,0:T(8,128)} %broadcast_in_dim.72), calls=%async_computation.1 | async-start | bytes 1048576 | tf_op jit(solution)/shard_map/lead_x/all_to_all | solution.py:189
  31.0 0.1 constant_dynamic-slice_fusion
  31.1 0.0 copy-start.3
  31.1 0.7 copy-done.3
  31.9 7.2 %all-to-all-done.1 = f32[4,2,64,256]{3,2,1,0:T(8,128)S(1)} async-done(((f32[4,2,64,256]{3,2,1,0:T(8,128)}), f32[4,2,64,256]{3,2,1,0:T(8,128)S(1)}, u32[]{:S(2)}, u32[]{:S(2)}) %all-to-all-start.1) | async-done | bytes 524320 | tf_op jit(solution)/shard_map/lead_x/all_to_all | solution.py:189
  39.1 0.0 copy-start.1
  39.1 0.8 copy-done.1
  40.0 1.9 %collective-permute-start = (f32[640,256]{1,0:T(8,128)S(1)}, f32[640,256]{1,0:T(8,128)S(1)}, u32[]{:S(2)}, u32[]{:S(2)}) collective-permute-start(f32[640,256]{1,0:T(8,128)S(1)} %pad_maximum_fusion.mine_ref), channel_id=1, source_target_pairs={{0,1},{1,0},{8,9},{9,8},{16,17},{17,16},{24,25},{25,24},{32,33},{3... | collective-permute-start | bytes 1966088 | tf_op jit(solution)/shard_map/ppermute | solution.py:224
  41.9 0.8 copy.27
  42.7 0.9 broadcast_in_dim.78
  43.6 5.5 %all-to-all-start.2 = ((f32[8,64,256]{2,1,0:T(8,128)}), f32[8,64,256]{2,1,0:T(8,128)}, u32[]{:S(2)}, u32[]{:S(2)}) async-start(f32[8,64,256]{2,1,0:T(8,128)} %broadcast_in_dim.78), calls=%async_computation.2 | async-start | bytes 1048576 | tf_op jit(solution)/shard_map/rest_row/all_to_all | solution.py:189
  49.1 0.1 iota_compare_fusion
  49.2 0.0 collective-permute-done.other_ref
  49.2 13.4 %factor.1 = (f32[128,256]{1,0:T(8,128)S(1)}, f32[128,256]{1,0:T(8,128)}) custom-call(s32[1]{0:T(128)} %bitcast.first_ref, f32[640,256]{1,0:T(8,128)S(1)} %pad_maximum_fusion.mine_ref, f32[640,256]{1,0:T(8,128)S(1)} %collective-permute-done.other_ref), custom_call_target="tpu_custom_call" | custom-call | tf_op jit(solution)/shard_map/inverse/factor/pallas_call | solution.py:169
  62.6 4.9 %collective-permute-start.1 = (f32[128,256]{1,0:T(8,128)}, f32[128,256]{1,0:T(8,128)S(1)}, u32[]{:S(2)}, u32[]{:S(2)}) collective-permute-start(f32[128,256]{1,0:T(8,128)} %get-tuple-element.8), channel_id=1, source_target_pairs={{0,4},{1,5},{8,12},{9,13},{16,20},{17,21},{24,28},{25,29},{32,36},... | collective-permute-start | bytes 393224 | tf_op jit(solution)/shard_map/ppermute | solution.py:228
  67.5 0.0 copy-start.2
  67.5 3.1 %collective-permute-done.1 = f32[128,256]{1,0:T(8,128)S(1)} collective-permute-done((f32[128,256]{1,0:T(8,128)}, f32[128,256]{1,0:T(8,128)S(1)}, u32[]{:S(2)}, u32[]{:S(2)}) %collective-permute-start.1) | collective-permute-done | bytes 131104 | tf_op jit(solution)/shard_map/ppermute | solution.py:228
  70.6 1.6 %broadcast_select_fusion = f32[128,256]{1,0:T(8,128)} fusion(f32[128,256]{1,0:T(8,128)} %get-tuple-element.8, f32[128,256]{1,0:T(8,128)S(1)} %collective-permute-done.1, pred[]{:T(512)S(6)} %lt.45), kind=kLoop, calls=%fused_computation.15 | loop fusion | flops 32768 | bytes 393217 | tf_op jit(solution)/shard_map/jit(_where)/select_n | solution.py:229
  72.2 1.9 %collective-permute-start.2 = (f32[128,256]{1,0:T(8,128)}, f32[128,256]{1,0:T(8,128)}, u32[]{:S(2)}, u32[]{:S(2)}) collective-permute-start(f32[128,256]{1,0:T(8,128)} %broadcast_select_fusion), channel_id=1, source_target_pairs={{0,2},{1,3},{4,6},{5,7},{8,10},{9,11},{12,14},{13,15},{16,18},{17,... | collective-permute-start | bytes 393224 | tf_op jit(solution)/shard_map/ppermute | solution.py:230
  74.1 0.1 broadcast_compare_fusion.1
  74.2 0.0 all-to-all-done.2
  74.2 0.9 %slice.24 = f32[2,64,256]{2,1,0:T(8,128)S(1)} slice(f32[8,64,256]{2,1,0:T(8,128)} %all-to-all-done.2), slice={[0:2], [0:64], [0:256]} | slice | bytes 262144 | tf_op jit(solution)/shard_map/rest_row/slice | solution.py:214
  75.1 0.8 broadcast_in_dim.79
  76.0 3.5 %all-to-all-start.3 = ((f32[4,2,64,256]{3,2,1,0:T(8,128)}), f32[4,2,64,256]{3,2,1,0:T(8,128)S(1)}, u32[]{:S(2)}, u32[]{:S(2)}) async-start(f32[4,2,64,256]{3,2,1,0:T(8,128)} %broadcast_in_dim.79), calls=%async_computation.3 | async-start | bytes 1048576 | tf_op jit(solution)/shard_map/rest_x/all_to_all | solution.py:189
  79.4 0.0 copy-start.4
  79.4 0.0 collective-permute-done.2
  79.5 1.6 %broadcast_select_fusion.1 = f32[128,256]{1,0:T(8,128)} fusion(f32[128,256]{1,0:T(8,128)} %broadcast_select_fusion, f32[128,256]{1,0:T(8,128)} %collective-permute-done.2, pred[]{:T(512)S(6)} %lt.44), kind=kLoop, calls=%fused_computation.16 | loop fusion | flops 32768 | bytes 393217 | tf_op jit(solution)/shard_map/jit(_where)/select_n | solution.py:231
  81.1 1.9 %collective-permute-start.3 = (f32[128,256]{1,0:T(8,128)}, f32[128,256]{1,0:T(8,128)}, u32[]{:S(2)}, u32[]{:S(2)}) collective-permute-start(f32[128,256]{1,0:T(8,128)} %broadcast_select_fusion.1), channel_id=1, source_target_pairs={{0,1},{1,0},{2,3},{3,2},{4,5},{5,4},{6,7},{7,6},{8,9},{9,8},{10,11... | collective-permute-start | bytes 393224 | tf_op jit(solution)/shard_map/ppermute | solution.py:232
  83.0 0.5 broadcast_compare_fusion.3
  83.5 0.5 broadcast_compare_fusion.2
  84.1 3.4 %all-to-all-done.3 = f32[4,2,64,256]{3,2,1,0:T(8,128)S(1)} async-done(((f32[4,2,64,256]{3,2,1,0:T(8,128)}), f32[4,2,64,256]{3,2,1,0:T(8,128)S(1)}, u32[]{:S(2)}, u32[]{:S(2)}) %all-to-all-start.3) | async-done | bytes 524320 | tf_op jit(solution)/shard_map/rest_x/all_to_all | solution.py:189
  87.5 0.0 copy-start.5
  87.5 0.0 copy-start.6
  87.6 0.0 collective-permute-done.3
  87.6 1.0 %broadcast_select_fusion.3 = (f32[128,256]{1,0:T(8,128)S(1)}, f32[128,256]{1,0:T(8,128)S(1)}) fusion(f32[128,256]{1,0:T(8,128)} %broadcast_select_fusion.1, f32[128,256]{1,0:T(8,128)} %collective-permute-done.3, pred[]{:T(512)S(6)} %eq.25), kind=kLoop, calls=%fused_computation.18 | loop fusion | flops 65536 | bytes 524289 | tf_op jit(solution)/shard_map/jit(_where)/select_n | solution.py:235
  88.6 0.0 copy-done.2
  88.6 0.7 fusion
  89.3 0.2 reshape.141
  89.5 0.0 copy-done.4
  89.5 0.0 copy-done.5
  89.5 0.0 copy-done.6
  89.5 0.2 fusion.8
  89.7 1.0 %copy.10 = f32[4,1,32,2,1,256]{5,4,3,2,1,0:T(1,128)} copy(f32[4,1,32,2,1,256]{5,2,4,3,1,0:T(8,128)S(1)} %fusion.8) | data formatting | bytes 524288 | tf_op jit(solution)/shard_map/jit(_where)/select_n | solution.py:248
  (12 shorter events, 0.2 us)
Async XLA Ops:
  0.0 1.6 %copy-start = (f32[4,1,256,2,1,256]{5,4,3,2,1,0:T(1,128)S(1)}, f32[4,1,256,2,1,256]{5,4,3,2,1,0:T(1,128)}, u32[]{:S(2)}) copy-start(f32[4,1,256,2,1,256]{5,4,3,2,1,0:T(1,128)} %param.1) | copy-start | bytes 6291460
  26.7 12.4 %all-to-all-start.1 = ((f32[4,2,64,256]{3,2,1,0:T(8,128)}), f32[4,2,64,256]{3,2,1,0:T(8,128)S(1)}, u32[]{:S(2)}, u32[]{:S(2)}) async-start(f32[4,2,64,256]{3,2,1,0:T(8,128)} %broadcast_in_dim.72), calls=%async_computation.1 | async-start | bytes 1048576 | tf_op jit(solution)/shard_map/lead_x/all_to_all | solution.py:189
  31.1 0.7 copy-start.3
  39.1 0.8 copy-start.1
  40.0 9.2 %collective-permute-start = (f32[640,256]{1,0:T(8,128)S(1)}, f32[640,256]{1,0:T(8,128)S(1)}, u32[]{:S(2)}, u32[]{:S(2)}) collective-permute-start(f32[640,256]{1,0:T(8,128)S(1)} %pad_maximum_fusion.mine_ref), channel_id=1, source_target_pairs={{0,1},{1,0},{8,9},{9,8},{16,17},{17,16},{24,25},{25,24},{32,33},{3... | collective-permute-start | bytes 1966088 | tf_op jit(solution)/shard_map/ppermute | solution.py:224
  43.6 30.6 %all-to-all-start.2 = ((f32[8,64,256]{2,1,0:T(8,128)}), f32[8,64,256]{2,1,0:T(8,128)}, u32[]{:S(2)}, u32[]{:S(2)}) async-start(f32[8,64,256]{2,1,0:T(8,128)} %broadcast_in_dim.78), calls=%async_computation.2 | async-start | bytes 1048576 | tf_op jit(solution)/shard_map/rest_row/all_to_all | solution.py:189
  62.6 8.0 %collective-permute-start.1 = (f32[128,256]{1,0:T(8,128)}, f32[128,256]{1,0:T(8,128)S(1)}, u32[]{:S(2)}, u32[]{:S(2)}) collective-permute-start(f32[128,256]{1,0:T(8,128)} %get-tuple-element.8), channel_id=1, source_target_pairs={{0,4},{1,5},{8,12},{9,13},{16,20},{17,21},{24,28},{25,29},{32,36},... | collective-permute-start | bytes 393224 | tf_op jit(solution)/shard_map/ppermute | solution.py:228
  67.5 21.0 %copy-start.2 = (f32[2,4,64,256]{3,2,1,0:T(8,128)S(1)}, f32[2,4,64,256]{3,2,1,0:T(8,128)}, u32[]{:S(2)}) copy-start(f32[2,4,64,256]{3,2,1,0:T(8,128)} %copy-done.1) | copy-start | bytes 1572868
  72.2 7.3 %collective-permute-start.2 = (f32[128,256]{1,0:T(8,128)}, f32[128,256]{1,0:T(8,128)}, u32[]{:S(2)}, u32[]{:S(2)}) collective-permute-start(f32[128,256]{1,0:T(8,128)} %broadcast_select_fusion), channel_id=1, source_target_pairs={{0,2},{1,3},{4,6},{5,7},{8,10},{9,11},{12,14},{13,15},{16,18},{17,... | collective-permute-start | bytes 393224 | tf_op jit(solution)/shard_map/ppermute | solution.py:230
  76.0 11.5 %all-to-all-start.3 = ((f32[4,2,64,256]{3,2,1,0:T(8,128)}), f32[4,2,64,256]{3,2,1,0:T(8,128)S(1)}, u32[]{:S(2)}, u32[]{:S(2)}) async-start(f32[4,2,64,256]{3,2,1,0:T(8,128)} %broadcast_in_dim.79), calls=%async_computation.3 | async-start | bytes 1048576 | tf_op jit(solution)/shard_map/rest_x/all_to_all | solution.py:189
  79.4 10.0 %copy-start.4 = (f32[4,1,32,2,1,256]{5,4,3,2,1,0:T(1,128)S(1)}, f32[4,1,32,2,1,256]{5,4,3,2,1,0:T(1,128)}, u32[]{:S(2)}) copy-start(f32[4,1,32,2,1,256]{5,4,3,2,1,0:T(1,128)} %copy-done.3) | copy-start | bytes 786436
  81.1 6.5 %collective-permute-start.3 = (f32[128,256]{1,0:T(8,128)}, f32[128,256]{1,0:T(8,128)}, u32[]{:S(2)}, u32[]{:S(2)}) collective-permute-start(f32[128,256]{1,0:T(8,128)} %broadcast_select_fusion.1), channel_id=1, source_target_pairs={{0,1},{1,0},{2,3},{3,2},{4,5},{5,4},{6,7},{7,6},{8,9},{9,8},{10,11... | collective-permute-start | bytes 393224 | tf_op jit(solution)/shard_map/ppermute | solution.py:232
  87.5 1.9 %copy-start.5 = (pred[2]{0:T(512)(128)(4,1)S(1)}, pred[2]{0:T(512)(128)(4,1)}, u32[]{:S(2)}) copy-start(pred[2]{0:T(512)(128)(4,1)} %broadcast_compare_fusion.3) | copy-start | bytes 10
  87.5 1.9 %copy-start.6 = (pred[4]{0:T(512)(128)(4,1)S(1)}, pred[4]{0:T(512)(128)(4,1)}, u32[]{:S(2)}) copy-start(pred[4]{0:T(512)(128)(4,1)} %broadcast_compare_fusion.2) | copy-start | bytes 16

commit v5 on v4

--- a/solution.py
+++ b/solution.py
@@ -14,6 +14,7 @@
 
 def product(left, right, dims=((1,), (0,))):
     return lax.dot_general(left, right, (dims, ((), ())), precision=HIGHEST, preferred_element_type=jnp.float32)
+
 
 def spread_lane(part, lane, sublane):
     return jnp.where(sublane < 8, jnp.broadcast_to(part[:, lane : lane + 1], (8, 128)), 0.0)
@@ -68,13 +69,12 @@
     return jnp.concatenate(parts, axis=0)
 
 
-def factor_kernel(
-    first_ref, mine_ref, other_ref, panel_ref, half_ref, v_ref, x_ref, w_ref, p_ref, e_ref, block_ref
+def factor_body(
+    first, mine_ref, other_ref, panel_ref, half_ref, v_ref, x_ref, w_ref, p_ref, e_ref, block_ref
 ):
     size = w_ref.shape[0]
     half = size // 2
     count = size // BLOCK
-    first = first_ref[0] == 1
     def left(rows):
         return jnp.where(first, mine_ref[rows, :], other_ref[rows, :])
     def right(rows):
@@ -89,10 +89,8 @@
     pending = []
     for k in range(count):
         slots = 2 * STRIP // 8
-        done_slots = [0]
         per = -(-len(pending) // (slots - 2)) if pending else 0
         def work():
-            done_slots[0] += 1
             for _ in range(per):
                 if pending:
                     pending.pop(0)()
@@ -140,17 +138,17 @@
             bind = functools.partial
             for j in range(k + 2, count):
                 pending.append(bind(panel, j=j))
-            pending.append(bind(panel_p))
+            pending.append(panel_p)
             for i in range(k + 1, count):
                 for j in range(i, count):
                     if j > k + 1:
                         pending.append(bind(trail, i=i, j=j))
                 pending.append(bind(trail_p, i=i))
             if k > 0:
-                pending.append(bind(panel_e))
+                pending.append(panel_e)
             for i in range(k + 1, count):
                 pending.append(bind(trail_e, i=i))
-            pending.append(bind(output))
+            pending.append(output)
     last = at[count - 1]
     inverse = block_ref[...]
     solved = product(p_ref[last, :], inverse, ((0,), (1,)))
@@ -161,7 +159,21 @@
     panel_ref[...] = jnp.where(first, v_ref[:, :half], v_ref[:, half:])
     half_ref[...] = jnp.where(first, x_ref[:, :half], x_ref[:, half:])
 
-def weigh(first, mine, other):
+
+def factor_kernel(position_ref, mine_ref, other_ref, panel_ref, half_ref, *scratch):
+    position = position_ref[0]
+
+    @pl.when(position < 2)
+    def _():
+        factor_body(position == 0, mine_ref, other_ref, panel_ref, half_ref, *scratch)
+
+    @pl.when(position >= 2)
+    def _():
+        panel_ref[...] = jnp.zeros_like(panel_ref)
+        half_ref[...] = jnp.zeros_like(half_ref)
+
+
+def weigh(position, mine, other):
     size = 2 * mine.shape[1]
     share = mine.shape[0] - size
     shape = jax.ShapeDtypeStruct((share, size // 2), jnp.float32)
@@ -181,7 +193,7 @@
         ],
         compiler_params=pltpu.CompilerParams(vmem_limit_bytes=16 << 20),
         name="factor",
-    )(first, mine, other)
+    )(position, mine, other)
 
 
 def to_all(piece, axis, peers, groups=None):
@@ -209,22 +221,18 @@
         (0, 0, (layer_here // 2) * quarter, 0, 0, 0),
         (1, 1, quarter, col_blocks, 1, width),
     ).reshape(quarter, col_blocks, width)
-    def collect(part, name):
-        with jax.named_scope(name + "_row"):
-            quarters = to_all(part, "row", grid_rows)[:PANELS]
-        with jax.named_scope(name + "_x"):
-            gathered = to_all(quarters, "layer", x_size, x_groups)
+    def collect(part):
+        quarters = to_all(part, "row", grid_rows)[:PANELS]
+        gathered = to_all(quarters, "layer", x_size, x_groups)
         return jnp.moveaxis(gathered, 0, 1).reshape(lead, -1)
 
-    lead_part = collect(head[:, 0, :], "lead")
-    rest_part = collect(head[:, 1:, :].reshape(quarter, (col_blocks - 1) * width), "rest")
+    lead_part = collect(head[:, 0, :])
+    rest_part = collect(head[:, 1:, :].reshape(quarter, (col_blocks - 1) * width))
     mine = lax.dynamic_slice_in_dim(held, layer_here * share, share, 1)
     mine_first = mine[:, :, 0, :].reshape(row_blocks * share, width)
     swapped_in = jnp.concatenate([lead_part, mine_first], axis=0)
     swapped = lax.ppermute(swapped_in, "col", [(0, 1), (1, 0)])
-    is_first = col_here == 0
-    with jax.named_scope("inverse"):
-        panel, half = weigh(is_first.astype(jnp.int32)[None], swapped_in, swapped)
+    panel, half = weigh(col_here[None], swapped_in, swapped)
     far = lax.ppermute(half, "col", [(0, 4), (1, 5)])
     half = jnp.where(col_here < 4, half, far)
     near = lax.ppermute(half, "col", [(0, 2), (1, 3), (4, 6), (5, 7)])

time: 91.2 us -> 90 us (0.987)
  the two profiles are of different devices: /device:TPU:8 before, /device:TPU:1 now
where the time goes in v5:
time: 90 us; the launch traced here: 89.5 us
  starting transfers between devices  24.2 us (27%)
  blocking collectives  22.3 us (25%)
  Pallas kernels  13.4 us (15%)
  waiting for transfers between devices  13.2 us (15%)
  local copies, waits for them, and re-layouts  9.64 us (11%)
  other arithmetic  5.66 us (6%)
    all_to_all x1, blocking collectives, to_all(): return lax.all_to_all(copies, axis, 0, 0, axis_index_groups=groups)  22.3 us
    pallas_call x1, Pallas kernels, weigh(): pl.pallas_call(factor_kernel, out_shape=[shape, shape], in_specs=[pl.Bloc...  13.4 us
    all_to_all x3, starting transfers between devices, to_all(): return lax.all_to_all(copies, axis, 0, 0, axis_index_groups=groups)  12.9 us
    all_to_all x3, waiting for transfers between devices, to_all(): return lax.all_to_all(copies, axis, 0, 0, axis_index_groups=groups)  9.82 us
    ppermute x1, starting transfers between devices, local(): swapped = lax.ppermute(swapped_in, 'col', [(0, 1), (1, 0)])  5.67 us
    unnamed x18, local copies, waits for them, and re-layouts  4.03 us
    ppermute x1, waiting for transfers between devices, local(): far = lax.ppermute(half, 'col', [(0, 4), (1, 5)])  3.36 us
    broadcast_in_dim x4, local copies, waits for them, and re-layouts, to_all(): copies = jnp.broadcast_to(piece[None], (peers, *piece.shape))  2.57 us
  transfers between devices with their start and end apart: 7, of which 3 were waited for; matrix products, arithmetic and copies ran while one was open for 9% of the time, Pallas kernels for 15%

profile of v5, /device:TPU:1, one launch (start us, length us, event | category | flops | bytes accessed | tf_op | source)
XLA Modules:
  0.0 89.5 jit_solution(10861549619354299623)
XLA Ops:
  0.0 0.0 copy-start
  0.0 1.6 %copy-done = f32[4,1,256,2,1,256]{5,4,3,2,1,0:T(1,128)S(1)} copy-done((f32[4,1,256,2,1,256]{5,4,3,2,1,0:T(1,128)S(1)}, f32[4,1,256,2,1,256]{5,4,3,2,1,0:T(1,128)}, u32[]{:S(2)}) %copy-start) | copy-done | bytes 2097176
  1.6 0.1 copy.26
  1.7 0.7 fusion.10
  2.5 22.3 %all_to_all.20 = f32[8,64,256]{2,1,0:T(8,128)S(1)} all-to-all(f32[8,64,256]{2,1,0:T(8,128)S(1)} %broadcast_in_dim.68), channel_id=1, replica_groups=mesh['layer'=8,'row'=8,'col'=8] {'row'}, dimensions={0} | all-to-all | bytes 1048576 | tf_op jit(solution)/shard_map/all_to_all | solution.py:201
  24.8 0.8 broadcast_in_dim.69
  25.6 5.2 %all-to-all-start.1 = ((f32[4,2,64,256]{3,2,1,0:T(8,128)}), f32[4,2,64,256]{3,2,1,0:T(8,128)S(1)}, u32[]{:S(2)}, u32[]{:S(2)}) async-start(f32[4,2,64,256]{3,2,1,0:T(8,128)} %broadcast_in_dim.69), calls=%async_computation.1 | async-start | bytes 1048576 | tf_op jit(solution)/shard_map/all_to_all | solution.py:201
  30.9 0.1 constant_dynamic-slice_fusion
  31.0 0.0 copy-start.3
  31.0 0.7 copy-done.3
  31.8 6.0 %all-to-all-done.1 = f32[4,2,64,256]{3,2,1,0:T(8,128)S(1)} async-done(((f32[4,2,64,256]{3,2,1,0:T(8,128)}), f32[4,2,64,256]{3,2,1,0:T(8,128)S(1)}, u32[]{:S(2)}, u32[]{:S(2)}) %all-to-all-start.1) | async-done | bytes 524320 | tf_op jit(solution)/shard_map/all_to_all | solution.py:201
  37.9 0.0 copy-start.1
  37.9 0.8 copy-done.1
  38.7 5.7 %collective-permute-start = (f32[640,256]{1,0:T(8,128)S(1)}, f32[640,256]{1,0:T(8,128)S(1)}, u32[]{:S(2)}, u32[]{:S(2)}) collective-permute-start(f32[640,256]{1,0:T(8,128)S(1)} %pad_maximum_fusion.mine_ref), channel_id=1, source_target_pairs={{0,1},{1,0},{8,9},{9,8},{16,17},{17,16},{24,25},{25,24},{32,33},{3... | collective-permute-start | bytes 1966088 | tf_op jit(solution)/shard_map/ppermute | solution.py:234
  44.4 0.8 copy.27
  45.2 0.9 broadcast_in_dim.75
  46.1 4.2 %all-to-all-start.2 = ((f32[8,64,256]{2,1,0:T(8,128)}), f32[8,64,256]{2,1,0:T(8,128)}, u32[]{:S(2)}, u32[]{:S(2)}) async-start(f32[8,64,256]{2,1,0:T(8,128)} %broadcast_in_dim.75), calls=%async_computation.2 | async-start | bytes 1048576 | tf_op jit(solution)/shard_map/all_to_all | solution.py:201
  50.3 0.1 iota_compare_fusion
  50.3 0.0 collective-permute-done.other_ref
  50.3 13.4 %factor.1 = (f32[128,256]{1,0:T(8,128)S(1)}, f32[128,256]{1,0:T(8,128)}) custom-call(s32[1]{0:T(128)} %bitcast.position_ref, f32[640,256]{1,0:T(8,128)S(1)} %pad_maximum_fusion.mine_ref, f32[640,256]{1,0:T(8,128)S(1)} %collective-permute-done.other_ref), custom_call_target="tpu_custom_call" | custom-call | tf_op jit(solution)/shard_map/factor/pallas_call | solution.py:181
  63.8 1.3 %collective-permute-start.1 = (f32[128,256]{1,0:T(8,128)}, f32[128,256]{1,0:T(8,128)S(1)}, u32[]{:S(2)}, u32[]{:S(2)}) collective-permute-start(f32[128,256]{1,0:T(8,128)} %get-tuple-element.8), channel_id=1, source_target_pairs={{0,4},{1,5},{8,12},{9,13},{16,20},{17,21},{24,28},{25,29},{32,36},... | collective-permute-start | bytes 393224 | tf_op jit(solution)/shard_map/ppermute | solution.py:236
  65.1 0.0 copy-start.2
  65.1 3.4 %collective-permute-done.1 = f32[128,256]{1,0:T(8,128)S(1)} collective-permute-done((f32[128,256]{1,0:T(8,128)}, f32[128,256]{1,0:T(8,128)S(1)}, u32[]{:S(2)}, u32[]{:S(2)}) %collective-permute-start.1) | collective-permute-done | bytes 131104 | tf_op jit(solution)/shard_map/ppermute | solution.py:236
  68.5 1.6 %broadcast_select_fusion = f32[128,256]{1,0:T(8,128)} fusion(f32[128,256]{1,0:T(8,128)} %get-tuple-element.8, f32[128,256]{1,0:T(8,128)S(1)} %collective-permute-done.1, pred[]{:T(512)S(6)} %lt.45), kind=kLoop, calls=%fused_computation.15 | loop fusion | flops 32768 | bytes 393217 | tf_op jit(solution)/shard_map/jit(_where)/select_n | solution.py:237
  70.1 1.9 %collective-permute-start.2 = (f32[128,256]{1,0:T(8,128)}, f32[128,256]{1,0:T(8,128)}, u32[]{:S(2)}, u32[]{:S(2)}) collective-permute-start(f32[128,256]{1,0:T(8,128)} %broadcast_select_fusion), channel_id=1, source_target_pairs={{0,2},{1,3},{4,6},{5,7},{8,10},{9,11},{12,14},{13,15},{16,18},{17,... | collective-permute-start | bytes 393224 | tf_op jit(solution)/shard_map/ppermute | solution.py:238
  72.0 0.1 broadcast_compare_fusion.1
  72.1 0.0 all-to-all-done.2
  72.1 0.9 %slice.24 = f32[2,64,256]{2,1,0:T(8,128)S(1)} slice(f32[8,64,256]{2,1,0:T(8,128)} %all-to-all-done.2), slice={[0:2], [0:64], [0:256]} | slice | bytes 262144 | tf_op jit(solution)/shard_map/slice | solution.py:225
  73.0 0.8 broadcast_in_dim.76
  73.9 3.5 %all-to-all-start.3 = ((f32[4,2,64,256]{3,2,1,0:T(8,128)}), f32[4,2,64,256]{3,2,1,0:T(8,128)S(1)}, u32[]{:S(2)}, u32[]{:S(2)}) async-start(f32[4,2,64,256]{3,2,1,0:T(8,128)} %broadcast_in_dim.76), calls=%async_computation.3 | async-start | bytes 1048576 | tf_op jit(solution)/shard_map/all_to_all | solution.py:201
  77.3 0.0 copy-start.4
  77.3 0.0 collective-permute-done.2
  77.4 1.6 %broadcast_select_fusion.1 = f32[128,256]{1,0:T(8,128)} fusion(f32[128,256]{1,0:T(8,128)} %broadcast_select_fusion, f32[128,256]{1,0:T(8,128)} %collective-permute-done.2, pred[]{:T(512)S(6)} %lt.44), kind=kLoop, calls=%fused_computation.16 | loop fusion | flops 32768 | bytes 393217 | tf_op jit(solution)/shard_map/jit(_where)/select_n | solution.py:239
  79.0 2.5 %collective-permute-start.3 = (f32[128,256]{1,0:T(8,128)}, f32[128,256]{1,0:T(8,128)}, u32[]{:S(2)}, u32[]{:S(2)}) collective-permute-start(f32[128,256]{1,0:T(8,128)} %broadcast_select_fusion.1), channel_id=1, source_target_pairs={{0,1},{1,0},{2,3},{3,2},{4,5},{5,4},{6,7},{7,6},{8,9},{9,8},{10,11... | collective-permute-start | bytes 393224 | tf_op jit(solution)/shard_map/ppermute | solution.py:240
  81.5 0.5 broadcast_compare_fusion.3
  82.0 0.5 broadcast_compare_fusion.2
  82.5 3.8 %all-to-all-done.3 = f32[4,2,64,256]{3,2,1,0:T(8,128)S(1)} async-done(((f32[4,2,64,256]{3,2,1,0:T(8,128)}), f32[4,2,64,256]{3,2,1,0:T(8,128)S(1)}, u32[]{:S(2)}, u32[]{:S(2)}) %all-to-all-start.3) | async-done | bytes 524320 | tf_op jit(solution)/shard_map/all_to_all | solution.py:201
  86.3 0.0 copy-start.5
  86.3 0.0 copy-start.6
  86.4 0.0 collective-permute-done.3
  86.4 1.0 %broadcast_select_fusion.3 = (f32[128,256]{1,0:T(8,128)S(1)}, f32[128,256]{1,0:T(8,128)S(1)}) fusion(f32[128,256]{1,0:T(8,128)} %broadcast_select_fusion.1, f32[128,256]{1,0:T(8,128)} %collective-permute-done.3, pred[]{:T(512)S(6)} %eq.21), kind=kLoop, calls=%fused_computation.18 | loop fusion | flops 65536 | bytes 524289 | tf_op jit(solution)/shard_map/jit(_where)/select_n | solution.py:243
  87.4 0.0 copy-done.2
  87.4 0.7 fusion
  88.1 0.2 reshape.141
  88.3 0.0 copy-done.4
  88.3 0.0 copy-done.5
  88.3 0.0 copy-done.6
  88.3 0.2 fusion.8
  88.5 1.0 %copy.10 = f32[4,1,32,2,1,256]{5,4,3,2,1,0:T(1,128)} copy(f32[4,1,32,2,1,256]{5,2,4,3,1,0:T(8,128)S(1)} %fusion.8) | data formatting | bytes 524288 | tf_op jit(solution)/shard_map/jit(_where)/select_n | solution.py:256
  (12 shorter events, 0.2 us)
Async XLA Ops:
  0.0 1.6 %copy-start = (f32[4,1,256,2,1,256]{5,4,3,2,1,0:T(1,128)S(1)}, f32[4,1,256,2,1,256]{5,4,3,2,1,0:T(1,128)}, u32[]{:S(2)}) copy-start(f32[4,1,256,2,1,256]{5,4,3,2,1,0:T(1,128)} %param.1) | copy-start | bytes 6291460
  25.6 12.2 %all-to-all-start.1 = ((f32[4,2,64,256]{3,2,1,0:T(8,128)}), f32[4,2,64,256]{3,2,1,0:T(8,128)S(1)}, u32[]{:S(2)}, u32[]{:S(2)}) async-start(f32[4,2,64,256]{3,2,1,0:T(8,128)} %broadcast_in_dim.69), calls=%async_computation.1 | async-start | bytes 1048576 | tf_op jit(solution)/shard_map/all_to_all | solution.py:201
  31.0 0.7 copy-start.3
  37.9 0.8 copy-start.1
  38.7 11.6 %collective-permute-start = (f32[640,256]{1,0:T(8,128)S(1)}, f32[640,256]{1,0:T(8,128)S(1)}, u32[]{:S(2)}, u32[]{:S(2)}) collective-permute-start(f32[640,256]{1,0:T(8,128)S(1)} %pad_maximum_fusion.mine_ref), channel_id=1, source_target_pairs={{0,1},{1,0},{8,9},{9,8},{16,17},{17,16},{24,25},{25,24},{32,33},{3... | collective-permute-start | bytes 1966088 | tf_op jit(solution)/shard_map/ppermute | solution.py:234
  46.1 26.0 %all-to-all-start.2 = ((f32[8,64,256]{2,1,0:T(8,128)}), f32[8,64,256]{2,1,0:T(8,128)}, u32[]{:S(2)}, u32[]{:S(2)}) async-start(f32[8,64,256]{2,1,0:T(8,128)} %broadcast_in_dim.75), calls=%async_computation.2 | async-start | bytes 1048576 | tf_op jit(solution)/shard_map/all_to_all | solution.py:201
  63.8 4.7 %collective-permute-start.1 = (f32[128,256]{1,0:T(8,128)}, f32[128,256]{1,0:T(8,128)S(1)}, u32[]{:S(2)}, u32[]{:S(2)}) collective-permute-start(f32[128,256]{1,0:T(8,128)} %get-tuple-element.8), channel_id=1, source_target_pairs={{0,4},{1,5},{8,12},{9,13},{16,20},{17,21},{24,28},{25,29},{32,36},... | collective-permute-start | bytes 393224 | tf_op jit(solution)/shard_map/ppermute | solution.py:236
  65.1 22.2 %copy-start.2 = (f32[2,4,64,256]{3,2,1,0:T(8,128)S(1)}, f32[2,4,64,256]{3,2,1,0:T(8,128)}, u32[]{:S(2)}) copy-start(f32[2,4,64,256]{3,2,1,0:T(8,128)} %copy-done.1) | copy-start | bytes 1572868
  70.1 7.3 %collective-permute-start.2 = (f32[128,256]{1,0:T(8,128)}, f32[128,256]{1,0:T(8,128)}, u32[]{:S(2)}, u32[]{:S(2)}) collective-permute-start(f32[128,256]{1,0:T(8,128)} %broadcast_select_fusion), channel_id=1, source_target_pairs={{0,2},{1,3},{4,6},{5,7},{8,10},{9,11},{12,14},{13,15},{16,18},{17,... | collective-permute-start | bytes 393224 | tf_op jit(solution)/shard_map/ppermute | solution.py:238
  73.9 12.4 %all-to-all-start.3 = ((f32[4,2,64,256]{3,2,1,0:T(8,128)}), f32[4,2,64,256]{3,2,1,0:T(8,128)S(1)}, u32[]{:S(2)}, u32[]{:S(2)}) async-start(f32[4,2,64,256]{3,2,1,0:T(8,128)} %broadcast_in_dim.76), calls=%async_computation.3 | async-start | bytes 1048576 | tf_op jit(solution)/shard_map/all_to_all | solution.py:201
  77.3 10.9 %copy-start.4 = (f32[4,1,32,2,1,256]{5,4,3,2,1,0:T(1,128)S(1)}, f32[4,1,32,2,1,256]{5,4,3,2,1,0:T(1,128)}, u32[]{:S(2)}) copy-start(f32[4,1,32,2,1,256]{5,4,3,2,1,0:T(1,128)} %copy-done.3) | copy-start | bytes 786436
  79.0 7.4 %collective-permute-start.3 = (f32[128,256]{1,0:T(8,128)}, f32[128,256]{1,0:T(8,128)}, u32[]{:S(2)}, u32[]{:S(2)}) collective-permute-start(f32[128,256]{1,0:T(8,128)} %broadcast_select_fusion.1), channel_id=1, source_target_pairs={{0,1},{1,0},{2,3},{3,2},{4,5},{5,4},{6,7},{7,6},{8,9},{9,8},{10,11... | collective-permute-start | bytes 393224 | tf_op jit(solution)/shard_map/ppermute | solution.py:240
  86.3 1.9 %copy-start.5 = (pred[2]{0:T(512)(128)(4,1)S(1)}, pred[2]{0:T(512)(128)(4,1)}, u32[]{:S(2)}) copy-start(pred[2]{0:T(512)(128)(4,1)} %broadcast_compare_fusion.3) | copy-start | bytes 10
  86.3 1.9 %copy-start.6 = (pred[4]{0:T(512)(128)(4,1)S(1)}, pred[4]{0:T(512)(128)(4,1)}, u32[]{:S(2)}) copy-start(pred[4]{0:T(512)(128)(4,1)} %broadcast_compare_fusion.2) | copy-start | bytes 16

commit v6 on v5

--- a/solution.py
+++ b/solution.py
@@ -196,6 +196,36 @@
     )(position, mine, other)
 
 
+def copies_kernel(start_ref, window_ref, lead_ref, rest_ref, part_ref, arrived):
+    rows = part_ref.shape[0]
+    begin = pl.multiple_of(start_ref[0] * rows, rows)
+    copy = pltpu.make_async_copy(window_ref.at[0, 0, pl.ds(begin, rows)], part_ref, arrived)
+    copy.start()
+    copy.wait()
+    for slot, out_ref in enumerate((lead_ref, rest_ref)):
+        part = part_ref[:, slot, 0, :]
+        for peer in range(out_ref.shape[0]):
+            out_ref[peer] = part
+
+
+def copies(start, window, peers, rows):
+    slots, width = window.shape[3], window.shape[5]
+    shape = jax.ShapeDtypeStruct((peers, rows, width), jnp.float32)
+    whole = pl.BlockSpec(memory_space=pltpu.VMEM)
+    return pl.pallas_call(
+        copies_kernel,
+        out_shape=[shape, shape],
+        in_specs=[pl.BlockSpec(memory_space=pltpu.SMEM), pl.BlockSpec(memory_space=pltpu.HBM)],
+        out_specs=[whole, whole],
+        scratch_shapes=[
+            pltpu.VMEM((rows, slots, 1, width), jnp.float32),
+            pltpu.SemaphoreType.DMA,
+        ],
+        compiler_params=pltpu.CompilerParams(vmem_limit_bytes=65500000),
+        name="copies",
+    )(start[None], window)
+
+
 def to_all(piece, axis, peers, groups=None):
     copies = jnp.broadcast_to(piece[None], (peers, *piece.shape))
     return lax.all_to_all(copies, axis, 0, 0, axis_index_groups=groups)
@@ -216,18 +246,15 @@
     quarter = width // x_size
     lead = PANELS * width
 
-    head = lax.dynamic_slice(
-        schur_window,
-        (0, 0, (layer_here // 2) * quarter, 0, 0, 0),
-        (1, 1, quarter, col_blocks, 1, width),
-    ).reshape(quarter, col_blocks, width)
+    parts = copies(layer_here // 2, schur_window, grid_rows, quarter)
+
     def collect(part):
-        quarters = to_all(part, "row", grid_rows)[:PANELS]
+        quarters = lax.all_to_all(part, "row", 0, 0)[:PANELS]
         gathered = to_all(quarters, "layer", x_size, x_groups)
         return jnp.moveaxis(gathered, 0, 1).reshape(lead, -1)
 
-    lead_part = collect(head[:, 0, :])
-    rest_part = collect(head[:, 1:, :].reshape(quarter, (col_blocks - 1) * width))
+    lead_part = collect(parts[0])
+    rest_part = collect(parts[1])
     mine = lax.dynamic_slice_in_dim(held, layer_here * share, share, 1)
     mine_first = mine[:, :, 0, :].reshape(row_blocks * share, width)
     swapped_in = jnp.concatenate([lead_part, mine_first], axis=0)

time: 90 us -> 82.4 us (0.916); the launches traced: 89.5 us -> 80.9 us
  local copies, waits for them, and re-layouts: 9.64 us -> 4.03 us
  other arithmetic: 5.66 us -> 0.49 us
  waiting for transfers between devices: 13.2 us -> 15.2 us
  Pallas kernels: 13.4 us -> 14.7 us
    unnamed x18 -> x1, local copies, waits for them, and re-layouts: 4.03 us -> 0.02 us
    all_to_all x3 -> x2, starting transfers between devices: 12.9 us -> 9.11 us  [to_all(): return lax.all_to_all(copies, axis, 0, 0, axis_index_groups=groups)]
    all_to_all x0 -> x1, starting transfers between devices: none -> 3.5 us  [collect(): quarters = lax.all_to_all(part, 'row', 0, 0)[:PANELS]]
    all_to_all x3 -> x2, waiting for transfers between devices: 9.82 us -> 12.2 us  [to_all(): return lax.all_to_all(copies, axis, 0, 0, axis_index_groups=groups)]
    pallas_call x0 -> x1, Pallas kernels: none -> 1.92 us  [copies(): pl.pallas_call(copies_kernel, out_shape=[shape, shape], in_specs=[pl.Bloc...]
    slice x3 -> x2, local copies, waits for them, and re-layouts: 1.65 us -> 0.02 us  [collect(): quarters = lax.all_to_all(part, 'row', 0, 0)[:PANELS]]
    select_n x1, other arithmetic: 1.64 us -> 0.02 us  [local(): half = jnp.where(col_here % 4 < 2, half, near)]
    select_n x1, other arithmetic: 1.59 us -> 0.02 us  [local(): half = jnp.where(col_here < 4, half, far)]
  transfers between devices with their start and end apart: 7 -> 7, of which waited for: 3 -> 3; matrix products, arithmetic and copies ran while one was open for 9% -> 3% of each run, Pallas kernels for 15% -> 16%
where the time goes in v6:
time: 82.4 us; the launch traced here: 80.9 us
  starting transfers between devices  23.4 us (28%)
  blocking collectives  22.1 us (27%)
  waiting for transfers between devices  15.2 us (18%)
  Pallas kernels  14.7 us (18%)
  local copies, waits for them, and re-layouts  4.03 us (5%)
    all_to_all x1, blocking collectives, collect(): quarters = lax.all_to_all(part, 'row', 0, 0)[:PANELS]  22.1 us
    pallas_call x1, Pallas kernels, weigh(): pl.pallas_call(factor_kernel, out_shape=[shape, shape], in_specs=[pl.Bloc...  12.8 us
    all_to_all x2, waiting for transfers between devices, to_all(): return lax.all_to_all(copies, axis, 0, 0, axis_index_groups=groups)  12.2 us
    all_to_all x2, starting transfers between devices, to_all(): return lax.all_to_all(copies, axis, 0, 0, axis_index_groups=groups)  9.11 us
    ppermute x1, starting transfers between devices, local(): swapped = lax.ppermute(swapped_in, 'col', [(0, 1), (1, 0)])  5.67 us
    all_to_all x1, starting transfers between devices, collect(): quarters = lax.all_to_all(part, 'row', 0, 0)[:PANELS]  3.5 us
    ppermute x1, waiting for transfers between devices, local(): far = lax.ppermute(half, 'col', [(0, 4), (1, 5)])  3.05 us
    ppermute x1, starting transfers between devices, local(): other = lax.ppermute(half, 'col', [(i, i ^ 1) for i in range(grid_cols)])  2.5 us
  transfers between devices with their start and end apart: 7, of which 3 were waited for; matrix products, arithmetic and copies ran while one was open for 3% of the time, Pallas kernels for 16%

profile of v6, /device:TPU:1, one launch (start us, length us, event | category | flops | bytes accessed | tf_op | source)
XLA Modules:
  0.0 80.9 jit_solution(10217889203883310138)
XLA Ops:
  0.0 1.9 %copies.1 = (f32[8,64,256]{2,1,0:T(8,128)}, f32[8,64,256]{2,1,0:T(8,128)}) custom-call(s32[1]{0:T(128)} %bitcast.1.start_ref, f32[4,1,256,2,1,256]{5,4,3,2,1,0:T(1,128)} %window_ref.1), custom_call_target="tpu_custom_call" | custom-call | tf_op jit(solution)/shard_map/copies/pallas_call | solution.py:215
  1.9 22.1 %all_to_all.20 = f32[8,64,256]{2,1,0:T(8,128)S(1)} all-to-all(f32[8,64,256]{2,1,0:T(8,128)} %get-tuple-element.9), channel_id=1, replica_groups=mesh['layer'=8,'row'=8,'col'=8] {'row'}, dimensions={0} | all-to-all | bytes 1048576 | tf_op jit(solution)/shard_map/all_to_all | solution.py:252
  24.1 0.8 %broadcast_in_dim.57 = f32[4,2,64,256]{3,2,1,0:T(8,128)} broadcast(f32[2,64,256]{2,1,0:T(8,128)S(1)} %slice.12), dimensions={1,2,3} | broadcast | bytes 655360 | tf_op jit(solution)/shard_map/broadcast_in_dim | solution.py:230
  24.9 5.6 %all-to-all-start.1 = ((f32[4,2,64,256]{3,2,1,0:T(8,128)}), f32[4,2,64,256]{3,2,1,0:T(8,128)S(1)}, u32[]{:S(2)}, u32[]{:S(2)}) async-start(f32[4,2,64,256]{3,2,1,0:T(8,128)} %broadcast_in_dim.57), calls=%async_computation.1 | async-start | bytes 1048576 | tf_op jit(solution)/shard_map/all_to_all | solution.py:231
  30.6 1.1 %constant_dynamic-slice_fusion = f32[4,1,32,2,1,256]{5,4,3,2,1,0:T(1,128)S(1)} fusion(f32[4,1,256,2,1,256]{5,4,3,2,1,0:T(1,128)} %window_ref.1, s32[]{:T(128)S(6)} %select_n.64), kind=kLoop, calls=%fused_computation.23 | loop fusion | bytes 524292 | tf_op jit(solution)/shard_map/dynamic_slice | solution.py:258
  31.7 5.8 %all-to-all-done.1 = f32[4,2,64,256]{3,2,1,0:T(8,128)S(1)} async-done(((f32[4,2,64,256]{3,2,1,0:T(8,128)}), f32[4,2,64,256]{3,2,1,0:T(8,128)S(1)}, u32[]{:S(2)}, u32[]{:S(2)}) %all-to-all-start.1) | async-done | bytes 524320 | tf_op jit(solution)/shard_map/all_to_all | solution.py:231
  37.6 5.7 %collective-permute-start = (f32[640,256]{1,0:T(8,128)S(1)}, f32[640,256]{1,0:T(8,128)S(1)}, u32[]{:S(2)}, u32[]{:S(2)}) collective-permute-start(f32[640,256]{1,0:T(8,128)S(1)} %pad_maximum_fusion.mine_ref), channel_id=1, source_target_pairs={{0,1},{1,0},{8,9},{9,8},{16,17},{17,16},{24,25},{25,24},{32,33},{3... | collective-permute-start | bytes 1966088 | tf_op jit(solution)/shard_map/ppermute | solution.py:261
  43.3 3.5 %all-to-all-start.2 = ((f32[8,64,256]{2,1,0:T(8,128)}), f32[8,64,256]{2,1,0:T(8,128)S(1)}, u32[]{:S(2)}, u32[]{:S(2)}) async-start(f32[8,64,256]{2,1,0:T(8,128)} %get-tuple-element.12), calls=%async_computation.2 | async-start | bytes 1048576 | tf_op jit(solution)/shard_map/all_to_all | solution.py:252
  46.8 0.1 iota_compare_fusion
  46.9 0.0 collective-permute-done.other_ref
  46.9 12.8 %factor.1 = (f32[128,256]{1,0:T(8,128)S(1)}, f32[128,256]{1,0:T(8,128)S(1)}) custom-call(s32[1]{0:T(128)} %bitcast.position_ref, f32[640,256]{1,0:T(8,128)S(1)} %pad_maximum_fusion.mine_ref, f32[640,256]{1,0:T(8,128)S(1)} %collective-permute-done.other_ref), custom_call_target="tpu_custom_call" | custom-call | tf_op jit(solution)/shard_map/factor/pallas_call | solution.py:181
  59.7 1.3 %collective-permute-start.1 = (f32[128,256]{1,0:T(8,128)S(1)}, f32[128,256]{1,0:T(8,128)S(1)}, u32[]{:S(2)}, u32[]{:S(2)}) collective-permute-start(f32[128,256]{1,0:T(8,128)S(1)} %get-tuple-element.11), channel_id=1, source_target_pairs={{0,4},{1,5},{8,12},{9,13},{16,20},{17,21},{24,28},{25,29},{32,36},... | collective-permute-start | bytes 393224 | tf_op jit(solution)/shard_map/ppermute | solution.py:263
  61.0 3.1 %collective-permute-done.1 = f32[128,256]{1,0:T(8,128)S(1)} collective-permute-done((f32[128,256]{1,0:T(8,128)S(1)}, f32[128,256]{1,0:T(8,128)S(1)}, u32[]{:S(2)}, u32[]{:S(2)}) %collective-permute-start.1) | collective-permute-done | bytes 131104 | tf_op jit(solution)/shard_map/ppermute | solution.py:263
  64.1 1.3 %collective-permute-start.2 = (f32[128,256]{1,0:T(8,128)S(1)}, f32[128,256]{1,0:T(8,128)S(1)}, u32[]{:S(2)}, u32[]{:S(2)}) collective-permute-start(f32[128,256]{1,0:T(8,128)S(1)} %broadcast_select_fusion), channel_id=1, source_target_pairs={{0,2},{1,3},{4,6},{5,7},{8,10},{9,11},{12,14},{13,15},{16,18},{17,... | collective-permute-start | bytes 393224 | tf_op jit(solution)/shard_map/ppermute | solution.py:265
  65.4 0.1 broadcast_compare_fusion.1
  65.5 0.0 all-to-all-done.2
  65.5 0.8 %broadcast_in_dim.62 = f32[4,2,64,256]{3,2,1,0:T(8,128)} broadcast(f32[2,64,256]{2,1,0:T(8,128)S(1)} %slice.14), dimensions={1,2,3} | broadcast | bytes 655360 | tf_op jit(solution)/shard_map/broadcast_in_dim | solution.py:230
  66.3 3.5 %all-to-all-start.3 = ((f32[4,2,64,256]{3,2,1,0:T(8,128)}), f32[4,2,64,256]{3,2,1,0:T(8,128)S(1)}, u32[]{:S(2)}, u32[]{:S(2)}) async-start(f32[4,2,64,256]{3,2,1,0:T(8,128)} %broadcast_in_dim.62), calls=%async_computation.3 | async-start | bytes 1048576 | tf_op jit(solution)/shard_map/all_to_all | solution.py:231
  69.8 0.0 collective-permute-done.2
  69.8 2.5 %collective-permute-start.3 = (f32[128,256]{1,0:T(8,128)S(1)}, f32[128,256]{1,0:T(8,128)S(1)}, u32[]{:S(2)}, u32[]{:S(2)}) collective-permute-start(f32[128,256]{1,0:T(8,128)S(1)} %broadcast_select_fusion.1), channel_id=1, source_target_pairs={{0,1},{1,0},{2,3},{3,2},{4,5},{5,4},{6,7},{7,6},{8,9},{9,8},{10,11... | collective-permute-start | bytes 393224 | tf_op jit(solution)/shard_map/ppermute | solution.py:267
  72.4 6.4 %all-to-all-done.3 = f32[4,2,64,256]{3,2,1,0:T(8,128)S(1)} async-done(((f32[4,2,64,256]{3,2,1,0:T(8,128)}), f32[4,2,64,256]{3,2,1,0:T(8,128)S(1)}, u32[]{:S(2)}, u32[]{:S(2)}) %all-to-all-start.3) | async-done | bytes 524320 | tf_op jit(solution)/shard_map/all_to_all | solution.py:231
  78.8 0.0 collective-permute-done.3
  78.8 0.7 fusion
  79.5 0.2 reshape.135
  79.7 0.2 fusion.8
  79.9 1.0 %copy.10 = f32[4,1,32,2,1,256]{5,4,3,2,1,0:T(1,128)} copy(f32[4,1,32,2,1,256]{5,2,4,3,1,0:T(8,128)S(1)} %fusion.8) | data formatting | bytes 524288 | tf_op jit(solution)/shard_map/jit(_where)/select_n | solution.py:283
  (15 shorter events, 0.3 us)
Async XLA Ops:
  24.9 12.6 %all-to-all-start.1 = ((f32[4,2,64,256]{3,2,1,0:T(8,128)}), f32[4,2,64,256]{3,2,1,0:T(8,128)S(1)}, u32[]{:S(2)}, u32[]{:S(2)}) async-start(f32[4,2,64,256]{3,2,1,0:T(8,128)} %broadcast_in_dim.57), calls=%async_computation.1 | async-start | bytes 1048576 | tf_op jit(solution)/shard_map/all_to_all | solution.py:231
  37.6 9.3 %collective-permute-start = (f32[640,256]{1,0:T(8,128)S(1)}, f32[640,256]{1,0:T(8,128)S(1)}, u32[]{:S(2)}, u32[]{:S(2)}) collective-permute-start(f32[640,256]{1,0:T(8,128)S(1)} %pad_maximum_fusion.mine_ref), channel_id=1, source_target_pairs={{0,1},{1,0},{8,9},{9,8},{16,17},{17,16},{24,25},{25,24},{32,33},{3... | collective-permute-start | bytes 1966088 | tf_op jit(solution)/shard_map/ppermute | solution.py:261
  43.3 22.2 %all-to-all-start.2 = ((f32[8,64,256]{2,1,0:T(8,128)}), f32[8,64,256]{2,1,0:T(8,128)S(1)}, u32[]{:S(2)}, u32[]{:S(2)}) async-start(f32[8,64,256]{2,1,0:T(8,128)} %get-tuple-element.12), calls=%async_computation.2 | async-start | bytes 1048576 | tf_op jit(solution)/shard_map/all_to_all | solution.py:252
  59.7 4.4 %collective-permute-start.1 = (f32[128,256]{1,0:T(8,128)S(1)}, f32[128,256]{1,0:T(8,128)S(1)}, u32[]{:S(2)}, u32[]{:S(2)}) collective-permute-start(f32[128,256]{1,0:T(8,128)S(1)} %get-tuple-element.11), channel_id=1, source_target_pairs={{0,4},{1,5},{8,12},{9,13},{16,20},{17,21},{24,28},{25,29},{32,36},... | collective-permute-start | bytes 393224 | tf_op jit(solution)/shard_map/ppermute | solution.py:263
  64.1 5.7 %collective-permute-start.2 = (f32[128,256]{1,0:T(8,128)S(1)}, f32[128,256]{1,0:T(8,128)S(1)}, u32[]{:S(2)}, u32[]{:S(2)}) collective-permute-start(f32[128,256]{1,0:T(8,128)S(1)} %broadcast_select_fusion), channel_id=1, source_target_pairs={{0,2},{1,3},{4,6},{5,7},{8,10},{9,11},{12,14},{13,15},{16,18},{17,... | collective-permute-start | bytes 393224 | tf_op jit(solution)/shard_map/ppermute | solution.py:265
  66.3 12.4 %all-to-all-start.3 = ((f32[4,2,64,256]{3,2,1,0:T(8,128)}), f32[4,2,64,256]{3,2,1,0:T(8,128)S(1)}, u32[]{:S(2)}, u32[]{:S(2)}) async-start(f32[4,2,64,256]{3,2,1,0:T(8,128)} %broadcast_in_dim.62), calls=%async_computation.3 | async-start | bytes 1048576 | tf_op jit(solution)/shard_map/all_to_all | solution.py:231
  69.8 9.0 %collective-permute-start.3 = (f32[128,256]{1,0:T(8,128)S(1)}, f32[128,256]{1,0:T(8,128)S(1)}, u32[]{:S(2)}, u32[]{:S(2)}) collective-permute-start(f32[128,256]{1,0:T(8,128)S(1)} %broadcast_select_fusion.1), channel_id=1, source_target_pairs={{0,1},{1,0},{2,3},{3,2},{4,5},{5,4},{6,7},{7,6},{8,9},{9,8},{10,11... | collective-permute-start | bytes 393224 | tf_op jit(solution)/shard_map/ppermute | solution.py:267

commit v7 on v6

--- a/solution.py
+++ b/solution.py
@@ -248,13 +248,23 @@
 
     parts = copies(layer_here // 2, schur_window, grid_rows, quarter)
 
-    def collect(part):
-        quarters = lax.all_to_all(part, "row", 0, 0)[:PANELS]
+    def across_x(quarters):
         gathered = to_all(quarters, "layer", x_size, x_groups)
         return jnp.moveaxis(gathered, 0, 1).reshape(lead, -1)
 
-    lead_part = collect(parts[0])
-    rest_part = collect(parts[1])
+    quarters = lax.all_to_all(parts[0], "row", 0, 0)[:PANELS]
+    lead_part = across_x(quarters)
+    part = parts[1][0]
+    other = lax.ppermute(part, "row", [(0, 1), (1, 0)])
+    is_top = row_here == 0
+    quarters = jnp.stack([jnp.where(is_top, part, other), jnp.where(is_top, other, part)])
+    received = lax.ppermute(quarters, "row", [(0, 6), (1, 3)])
+    quarters = jnp.where(row_here < PANELS, quarters, received)
+    received = lax.ppermute(quarters, "row", [(0, 7), (1, 2), (6, 5), (3, 4)])
+    holds = (row_here < PANELS) | (row_here == 3) | (row_here == 6)
+    quarters = jnp.where(holds, quarters, received)
+    rest_part = across_x(quarters)
+
     mine = lax.dynamic_slice_in_dim(held, layer_here * share, share, 1)
     mine_first = mine[:, :, 0, :].reshape(row_blocks * share, width)
     swapped_in = jnp.concatenate([lead_part, mine_first], axis=0)

time: 82.4 us -> 82.6 us (level)
  blocking collectives: 22.1 us -> 0 us
  waiting for transfers between devices: 15.2 us -> 26.4 us
  starting transfers between devices: 23.4 us -> 32.7 us
  other arithmetic: 0.49 us -> 1.39 us
  local copies, waits for them, and re-layouts: 4.03 us -> 4.88 us
    all_to_all x1 -> x0, blocking collectives: 22.1 us -> none  [collect(): quarters = lax.all_to_all(part, 'row', 0, 0)[:PANELS]]
    all_to_all x1, waiting for transfers between devices: 0.01 us -> 9.55 us  [local(): quarters = lax.all_to_all(parts[0], 'row', 0, 0)[:PANELS]]
    ppermute x0 -> x3, starting transfers between devices: none -> 5.95 us  [the longest x1 3.36 us: local(): other = lax.ppermute(part, 'row', [(0, 1), (1, 0)])]
    all_to_all x1, starting transfers between devices: 3.5 us -> 7.65 us  [local(): quarters = lax.all_to_all(parts[0], 'row', 0, 0)[:PANELS]]
    all_to_all x2, waiting for transfers between devices: 12.2 us -> 15.1 us  [to_all(): return lax.all_to_all(copies, axis, 0, 0, axis_index_groups=groups)]
    ppermute x1, starting transfers between devices: 5.67 us -> 3.54 us  [local(): swapped = lax.ppermute(swapped_in, 'col', [(0, 1), (1, 0)])]
    all_to_all x2, starting transfers between devices: 9.11 us -> 10.5 us  [to_all(): return lax.all_to_all(copies, axis, 0, 0, axis_index_groups=groups)]
    ppermute x1, waiting for transfers between devices: 3.05 us -> 1.76 us  [local(): far = lax.ppermute(half, 'col', [(0, 4), (1, 5)])]
  transfers between devices with their start and end apart: 7 -> 10, of which waited for: 3 -> 4; matrix products, arithmetic and copies ran while one was open for 3% -> 6% of each run, Pallas kernels for 16% -> 16%
where the time goes in v7:
time: 82.6 us; the launch traced here: 81.1 us
  starting transfers between devices  32.7 us (40%)
  waiting for transfers between devices  26.4 us (32%)
  Pallas kernels  14.7 us (18%)
  local copies, waits for them, and re-layouts  4.88 us (6%)
  other arithmetic  1.39 us (2%)
    all_to_all x2, waiting for transfers between devices, to_all(): return lax.all_to_all(copies, axis, 0, 0, axis_index_groups=groups)  15.1 us
    pallas_call x1, Pallas kernels, weigh(): pl.pallas_call(factor_kernel, out_shape=[shape, shape], in_specs=[pl.Bloc...  12.8 us
    all_to_all x2, starting transfers between devices, to_all(): return lax.all_to_all(copies, axis, 0, 0, axis_index_groups=groups)  10.5 us
    all_to_all x1, waiting for transfers between devices, local(): quarters = lax.all_to_all(parts[0], 'row', 0, 0)[:PANELS]  9.55 us
    all_to_all x1, starting transfers between devices, local(): quarters = lax.all_to_all(parts[0], 'row', 0, 0)[:PANELS]  7.65 us
    ppermute x1, starting transfers between devices, local(): swapped = lax.ppermute(swapped_in, 'col', [(0, 1), (1, 0)])  3.54 us
    ppermute x1, starting transfers between devices, local(): other = lax.ppermute(part, 'row', [(0, 1), (1, 0)])  3.36 us
    ppermute x1, starting transfers between devices, local(): other = lax.ppermute(half, 'col', [(i, i ^ 1) for i in range(grid_cols)])  2.49 us
  transfers between devices with their start and end apart: 10, of which 4 were waited for; matrix products, arithmetic and copies ran while one was open for 6% of the time, Pallas kernels for 16%

profile of v7, /device:TPU:1, one launch (start us, length us, event | category | flops | bytes accessed | tf_op | source)
XLA Modules:
  0.0 81.1 jit_solution(4373005147207030560)
XLA Ops:
  0.0 1.9 %copies.1 = (f32[8,64,256]{2,1,0:T(8,128)}, f32[8,64,256]{2,1,0:T(8,128)}) custom-call(s32[1]{0:T(128)} %bitcast.1.start_ref, f32[4,1,256,2,1,256]{5,4,3,2,1,0:T(1,128)} %window_ref.1), custom_call_target="tpu_custom_call" | custom-call | tf_op jit(solution)/shard_map/copies/pallas_call | solution.py:215
  1.9 7.7 %all-to-all-start = ((f32[8,64,256]{2,1,0:T(8,128)}), f32[8,64,256]{2,1,0:T(8,128)S(1)}, u32[]{:S(2)}, u32[]{:S(2)}) async-start(f32[8,64,256]{2,1,0:T(8,128)} %get-tuple-element.9), calls=%async_computation | async-start | bytes 1048576 | tf_op jit(solution)/shard_map/all_to_all | solution.py:255
  9.6 0.8 %slice_bitcast_fusion = f32[64,256]{1,0:T(8,128)S(1)} fusion(f32[8,64,256]{2,1,0:T(8,128)} %get-tuple-element.12), kind=kLoop, calls=%fused_computation.15 | loop fusion | bytes 131072 | tf_op jit(solution)/shard_map/squeeze | solution.py:257
  10.4 3.4 %collective-permute-start.4 = (f32[64,256]{1,0:T(8,128)S(1)}, f32[64,256]{1,0:T(8,128)S(1)}, u32[]{:S(2)}, u32[]{:S(2)}) collective-permute-start(f32[64,256]{1,0:T(8,128)S(1)} %slice_bitcast_fusion), channel_id=1, source_target_pairs={{0,8},{8,0},{1,9},{9,1},{2,10},{10,2},{3,11},{11,3},{4,12},{12,4},... | collective-permute-start | bytes 196616 | tf_op jit(solution)/shard_map/ppermute | solution.py:258
  13.8 1.1 %constant_dynamic-slice_fusion = f32[4,1,32,2,1,256]{5,4,3,2,1,0:T(1,128)S(1)} fusion(f32[4,1,256,2,1,256]{5,4,3,2,1,0:T(1,128)} %window_ref.1, s32[]{:T(128)S(6)} %select_n.90), kind=kLoop, calls=%fused_computation.29 | loop fusion | bytes 524292 | tf_op jit(solution)/shard_map/dynamic_slice | solution.py:268
  15.0 9.5 %all-to-all-done = f32[8,64,256]{2,1,0:T(8,128)S(1)} async-done(((f32[8,64,256]{2,1,0:T(8,128)}), f32[8,64,256]{2,1,0:T(8,128)S(1)}, u32[]{:S(2)}, u32[]{:S(2)}) %all-to-all-start) | async-done | bytes 524320 | tf_op jit(solution)/shard_map/all_to_all | solution.py:255
  24.6 0.9 %broadcast_in_dim.57 = f32[4,2,64,256]{3,2,1,0:T(8,128)} broadcast(f32[2,64,256]{2,1,0:T(8,128)S(1)} %slice.12), dimensions={1,2,3} | broadcast | bytes 655360 | tf_op jit(solution)/shard_map/broadcast_in_dim | solution.py:230
  25.4 7.0 %all-to-all-start.1 = ((f32[4,2,64,256]{3,2,1,0:T(8,128)}), f32[4,2,64,256]{3,2,1,0:T(8,128)S(1)}, u32[]{:S(2)}, u32[]{:S(2)}) async-start(f32[4,2,64,256]{3,2,1,0:T(8,128)} %broadcast_in_dim.57), calls=%async_computation.1 | async-start | bytes 1048576 | tf_op jit(solution)/shard_map/all_to_all | solution.py:231
  32.4 0.1 iota_compare_fusion
  32.5 8.7 %all-to-all-done.1 = f32[4,2,64,256]{3,2,1,0:T(8,128)S(1)} async-done(((f32[4,2,64,256]{3,2,1,0:T(8,128)}), f32[4,2,64,256]{3,2,1,0:T(8,128)S(1)}, u32[]{:S(2)}, u32[]{:S(2)}) %all-to-all-start.1) | async-done | bytes 524320 | tf_op jit(solution)/shard_map/all_to_all | solution.py:231
  41.3 3.5 %collective-permute-start = (f32[640,256]{1,0:T(8,128)S(1)}, f32[640,256]{1,0:T(8,128)S(1)}, u32[]{:S(2)}, u32[]{:S(2)}) collective-permute-start(f32[640,256]{1,0:T(8,128)S(1)} %pad_maximum_fusion.mine_ref), channel_id=1, source_target_pairs={{0,1},{1,0},{8,9},{9,8},{16,17},{17,16},{24,25},{25,24},{32,33},{3... | collective-permute-start | bytes 1966088 | tf_op jit(solution)/shard_map/ppermute | solution.py:271
  44.9 0.0 collective-permute-done.4
  44.9 0.9 %select_bitcast_fusion.1 = (f32[1,64,256]{2,1,0:T(8,128)S(1)}, f32[1,64,256]{2,1,0:T(8,128)S(1)}) fusion(f32[64,256]{1,0:T(8,128)S(1)} %collective-permute-done.4, pred[]{:T(512)S(6)} %eq.33, f32[8,64,256]{2,1,0:T(8,128)} %get-tuple-element.12), kind=kLoop, calls=%fused_computation.14 | loop fusion | flops 32768 | bytes 262145 | tf_op jit(solution)/shard_map/stack | solution.py:260
  45.8 1.3 %collective-permute-start.5 = (f32[2,64,256]{2,1,0:T(8,128)S(1)}, f32[2,64,256]{2,1,0:T(8,128)S(1)}, u32[]{:S(2)}, u32[]{:S(2)}) collective-permute-start(f32[2,64,256]{2,1,0:T(8,128)S(1)} %pad_maximum_fusion.1), channel_id=1, source_target_pairs={{0,48},{8,24},{1,49},{9,25},{2,50},{10,26},{3,51},{11,27},{4,52},{... | collective-permute-start | bytes 393224 | tf_op jit(solution)/shard_map/ppermute | solution.py:261
  47.1 0.1 broadcast_compare_fusion.1
  47.1 0.0 collective-permute-done.other_ref
  47.2 12.8 %factor.1 = (f32[128,256]{1,0:T(8,128)S(1)}, f32[128,256]{1,0:T(8,128)S(1)}) custom-call(s32[1]{0:T(128)} %bitcast.position_ref, f32[640,256]{1,0:T(8,128)S(1)} %pad_maximum_fusion.mine_ref, f32[640,256]{1,0:T(8,128)S(1)} %collective-permute-done.other_ref), custom_call_target="tpu_custom_call" | custom-call | tf_op jit(solution)/shard_map/factor/pallas_call | solution.py:181
  59.9 1.3 %collective-permute-start.1 = (f32[128,256]{1,0:T(8,128)S(1)}, f32[128,256]{1,0:T(8,128)S(1)}, u32[]{:S(2)}, u32[]{:S(2)}) collective-permute-start(f32[128,256]{1,0:T(8,128)S(1)} %get-tuple-element.11), channel_id=1, source_target_pairs={{0,4},{1,5},{8,12},{9,13},{16,20},{17,21},{24,28},{25,29},{32,36},... | collective-permute-start | bytes 393224 | tf_op jit(solution)/shard_map/ppermute | solution.py:273
  61.2 0.0 collective-permute-done.5
  61.3 1.3 %collective-permute-start.6 = (f32[2,64,256]{2,1,0:T(8,128)S(1)}, f32[2,64,256]{2,1,0:T(8,128)S(1)}, u32[]{:S(2)}, u32[]{:S(2)}) collective-permute-start(f32[2,64,256]{2,1,0:T(8,128)S(1)} %broadcast_select_fusion), channel_id=1, source_target_pairs={{0,56},{8,16},{48,40},{24,32},{1,57},{9,17},{49,41},{25,33},{2,58}... | collective-permute-start | bytes 393224 | tf_op jit(solution)/shard_map/ppermute | solution.py:263
  62.6 1.8 %collective-permute-done.1 = f32[128,256]{1,0:T(8,128)S(1)} collective-permute-done((f32[128,256]{1,0:T(8,128)S(1)}, f32[128,256]{1,0:T(8,128)S(1)}, u32[]{:S(2)}, u32[]{:S(2)}) %collective-permute-start.1) | collective-permute-done | bytes 131104 | tf_op jit(solution)/shard_map/ppermute | solution.py:273
  64.3 1.3 %collective-permute-start.2 = (f32[128,256]{1,0:T(8,128)S(1)}, f32[128,256]{1,0:T(8,128)S(1)}, u32[]{:S(2)}, u32[]{:S(2)}) collective-permute-start(f32[128,256]{1,0:T(8,128)S(1)} %broadcast_select_fusion.2), channel_id=1, source_target_pairs={{0,2},{1,3},{4,6},{5,7},{8,10},{9,11},{12,14},{13,15},{16,18},{17,... | collective-permute-start | bytes 393224 | tf_op jit(solution)/shard_map/ppermute | solution.py:275
  65.7 0.0 collective-permute-done.6
  65.7 0.8 %broadcast_in_dim.62 = f32[4,2,64,256]{3,2,1,0:T(8,128)} broadcast(f32[2,64,256]{2,1,0:T(8,128)S(1)} %broadcast_select_fusion.1), dimensions={1,2,3} | broadcast | bytes 655360 | tf_op jit(solution)/shard_map/broadcast_in_dim | solution.py:230
  66.5 3.5 %all-to-all-start.2 = ((f32[4,2,64,256]{3,2,1,0:T(8,128)}), f32[4,2,64,256]{3,2,1,0:T(8,128)S(1)}, u32[]{:S(2)}, u32[]{:S(2)}) async-start(f32[4,2,64,256]{3,2,1,0:T(8,128)} %broadcast_in_dim.62), calls=%async_computation.2 | async-start | bytes 1048576 | tf_op jit(solution)/shard_map/all_to_all | solution.py:231
  70.0 0.0 collective-permute-done.2
  70.0 2.5 %collective-permute-start.3 = (f32[128,256]{1,0:T(8,128)S(1)}, f32[128,256]{1,0:T(8,128)S(1)}, u32[]{:S(2)}, u32[]{:S(2)}) collective-permute-start(f32[128,256]{1,0:T(8,128)S(1)} %broadcast_select_fusion.3), channel_id=1, source_target_pairs={{0,1},{1,0},{2,3},{3,2},{4,5},{5,4},{6,7},{7,6},{8,9},{9,8},{10,11... | collective-permute-start | bytes 393224 | tf_op jit(solution)/shard_map/ppermute | solution.py:277
  72.6 6.4 %all-to-all-done.2 = f32[4,2,64,256]{3,2,1,0:T(8,128)S(1)} async-done(((f32[4,2,64,256]{3,2,1,0:T(8,128)}), f32[4,2,64,256]{3,2,1,0:T(8,128)S(1)}, u32[]{:S(2)}, u32[]{:S(2)}) %all-to-all-start.2) | async-done | bytes 524320 | tf_op jit(solution)/shard_map/all_to_all | solution.py:231
  79.0 0.0 collective-permute-done.3
  79.1 0.7 fusion
  79.8 0.2 reshape.135
  80.0 0.2 fusion.8
  80.2 1.0 %copy.10 = f32[4,1,32,2,1,256]{5,4,3,2,1,0:T(1,128)} copy(f32[4,1,32,2,1,256]{5,2,4,3,1,0:T(8,128)S(1)} %fusion.8) | data formatting | bytes 524288 | tf_op jit(solution)/shard_map/jit(_where)/select_n | solution.py:293
  (17 shorter events, 0.3 us)
Async XLA Ops:
  1.9 22.6 %all-to-all-start = ((f32[8,64,256]{2,1,0:T(8,128)}), f32[8,64,256]{2,1,0:T(8,128)S(1)}, u32[]{:S(2)}, u32[]{:S(2)}) async-start(f32[8,64,256]{2,1,0:T(8,128)} %get-tuple-element.9), calls=%async_computation | async-start | bytes 1048576 | tf_op jit(solution)/shard_map/all_to_all | solution.py:255
  10.4 34.4 %collective-permute-start.4 = (f32[64,256]{1,0:T(8,128)S(1)}, f32[64,256]{1,0:T(8,128)S(1)}, u32[]{:S(2)}, u32[]{:S(2)}) collective-permute-start(f32[64,256]{1,0:T(8,128)S(1)} %slice_bitcast_fusion), channel_id=1, source_target_pairs={{0,8},{8,0},{1,9},{9,1},{2,10},{10,2},{3,11},{11,3},{4,12},{12,4},... | collective-permute-start | bytes 196616 | tf_op jit(solution)/shard_map/ppermute | solution.py:258
  25.4 15.8 %all-to-all-start.1 = ((f32[4,2,64,256]{3,2,1,0:T(8,128)}), f32[4,2,64,256]{3,2,1,0:T(8,128)S(1)}, u32[]{:S(2)}, u32[]{:S(2)}) async-start(f32[4,2,64,256]{3,2,1,0:T(8,128)} %broadcast_in_dim.57), calls=%async_computation.1 | async-start | bytes 1048576 | tf_op jit(solution)/shard_map/all_to_all | solution.py:231
  41.3 5.8 %collective-permute-start = (f32[640,256]{1,0:T(8,128)S(1)}, f32[640,256]{1,0:T(8,128)S(1)}, u32[]{:S(2)}, u32[]{:S(2)}) collective-permute-start(f32[640,256]{1,0:T(8,128)S(1)} %pad_maximum_fusion.mine_ref), channel_id=1, source_target_pairs={{0,1},{1,0},{8,9},{9,8},{16,17},{17,16},{24,25},{25,24},{32,33},{3... | collective-permute-start | bytes 1966088 | tf_op jit(solution)/shard_map/ppermute | solution.py:271
  45.8 15.5 %collective-permute-start.5 = (f32[2,64,256]{2,1,0:T(8,128)S(1)}, f32[2,64,256]{2,1,0:T(8,128)S(1)}, u32[]{:S(2)}, u32[]{:S(2)}) collective-permute-start(f32[2,64,256]{2,1,0:T(8,128)S(1)} %pad_maximum_fusion.1), channel_id=1, source_target_pairs={{0,48},{8,24},{1,49},{9,25},{2,50},{10,26},{3,51},{11,27},{4,52},{... | collective-permute-start | bytes 393224 | tf_op jit(solution)/shard_map/ppermute | solution.py:261
  59.9 4.4 %collective-permute-start.1 = (f32[128,256]{1,0:T(8,128)S(1)}, f32[128,256]{1,0:T(8,128)S(1)}, u32[]{:S(2)}, u32[]{:S(2)}) collective-permute-start(f32[128,256]{1,0:T(8,128)S(1)} %get-tuple-element.11), channel_id=1, source_target_pairs={{0,4},{1,5},{8,12},{9,13},{16,20},{17,21},{24,28},{25,29},{32,36},... | collective-permute-start | bytes 393224 | tf_op jit(solution)/shard_map/ppermute | solution.py:273
  61.3 4.4 %collective-permute-start.6 = (f32[2,64,256]{2,1,0:T(8,128)S(1)}, f32[2,64,256]{2,1,0:T(8,128)S(1)}, u32[]{:S(2)}, u32[]{:S(2)}) collective-permute-start(f32[2,64,256]{2,1,0:T(8,128)S(1)} %broadcast_select_fusion), channel_id=1, source_target_pairs={{0,56},{8,16},{48,40},{24,32},{1,57},{9,17},{49,41},{25,33},{2,58}... | collective-permute-start | bytes 393224 | tf_op jit(solution)/shard_map/ppermute | solution.py:263
  64.3 5.7 %collective-permute-start.2 = (f32[128,256]{1,0:T(8,128)S(1)}, f32[128,256]{1,0:T(8,128)S(1)}, u32[]{:S(2)}, u32[]{:S(2)}) collective-permute-start(f32[128,256]{1,0:T(8,128)S(1)} %broadcast_select_fusion.2), channel_id=1, source_target_pairs={{0,2},{1,3},{4,6},{5,7},{8,10},{9,11},{12,14},{13,15},{16,18},{17,... | collective-permute-start | bytes 393224 | tf_op jit(solution)/shard_map/ppermute | solution.py:275
  66.5 12.4 %all-to-all-start.2 = ((f32[4,2,64,256]{3,2,1,0:T(8,128)}), f32[4,2,64,256]{3,2,1,0:T(8,128)S(1)}, u32[]{:S(2)}, u32[]{:S(2)}) async-start(f32[4,2,64,256]{3,2,1,0:T(8,128)} %broadcast_in_dim.62), calls=%async_computation.2 | async-start | bytes 1048576 | tf_op jit(solution)/shard_map/all_to_all | solution.py:231
  70.0 9.0 %collective-permute-start.3 = (f32[128,256]{1,0:T(8,128)S(1)}, f32[128,256]{1,0:T(8,128)S(1)}, u32[]{:S(2)}, u32[]{:S(2)}) collective-permute-start(f32[128,256]{1,0:T(8,128)S(1)} %broadcast_select_fusion.3), channel_id=1, source_target_pairs={{0,1},{1,0},{2,3},{3,2},{4,5},{5,4},{6,7},{7,6},{8,9},{9,8},{10,11... | collective-permute-start | bytes 393224 | tf_op jit(solution)/shard_map/ppermute | solution.py:277

commit v8 on v7

--- a/solution.py
+++ b/solution.py
@@ -202,19 +202,19 @@
     copy = pltpu.make_async_copy(window_ref.at[0, 0, pl.ds(begin, rows)], part_ref, arrived)
     copy.start()
     copy.wait()
-    for slot, out_ref in enumerate((lead_ref, rest_ref)):
-        part = part_ref[:, slot, 0, :]
-        for peer in range(out_ref.shape[0]):
-            out_ref[peer] = part
+    rest_ref[...] = part_ref[:, 1, 0, :]
+    part = part_ref[:, 0, 0, :]
+    for peer in range(lead_ref.shape[0]):
+        lead_ref[peer] = part
 
 
 def copies(start, window, peers, rows):
     slots, width = window.shape[3], window.shape[5]
-    shape = jax.ShapeDtypeStruct((peers, rows, width), jnp.float32)
+    shapes = [(peers, rows, width), (rows, width)]
     whole = pl.BlockSpec(memory_space=pltpu.VMEM)
     return pl.pallas_call(
         copies_kernel,
-        out_shape=[shape, shape],
+        out_shape=[jax.ShapeDtypeStruct(shape, jnp.float32) for shape in shapes],
         in_specs=[pl.BlockSpec(memory_space=pltpu.SMEM), pl.BlockSpec(memory_space=pltpu.HBM)],
         out_specs=[whole, whole],
         scratch_shapes=[
@@ -254,7 +254,7 @@
 
     quarters = lax.all_to_all(parts[0], "row", 0, 0)[:PANELS]
     lead_part = across_x(quarters)
-    part = parts[1][0]
+    part = parts[1]
     other = lax.ppermute(part, "row", [(0, 1), (1, 0)])
     is_top = row_here == 0
     quarters = jnp.stack([jnp.where(is_top, part, other), jnp.where(is_top, other, part)])

time: 82.6 us -> 81.5 us (0.987)
  the two profiles are of different devices: /device:TPU:1 before, /device:TPU:384 now
where the time goes in v8:
time: 81.5 us; the launch traced here: 81 us
  waiting for transfers between devices  47 us (58%)
  starting transfers between devices  26.6 us (33%)
  local copies, waits for them, and re-layouts  4.06 us (5%)
  Pallas kernels  1.79 us (2%)
    all_to_all x2, waiting for transfers between devices, to_all(): return lax.all_to_all(copies, axis, 0, 0, axis_index_groups=groups)  17 us
    ppermute x1, waiting for transfers between devices, local(): far = lax.ppermute(half, 'col', [(0, 4), (1, 5)])  16.5 us
    all_to_all x1, waiting for transfers between devices, local(): quarters = lax.all_to_all(parts[0], 'row', 0, 0)[:PANELS]  12.4 us
    all_to_all x2, starting transfers between devices, to_all(): return lax.all_to_all(copies, axis, 0, 0, axis_index_groups=groups)  7.76 us
    all_to_all x1, starting transfers between devices, local(): quarters = lax.all_to_all(parts[0], 'row', 0, 0)[:PANELS]  7.11 us
    ppermute x1, starting transfers between devices, local(): other = lax.ppermute(part, 'row', [(0, 1), (1, 0)])  3.92 us
    ppermute x1, starting transfers between devices, local(): other = lax.ppermute(half, 'col', [(i, i ^ 1) for i in range(grid_cols)])  1.92 us
    pallas_call x1, Pallas kernels, copies(): pl.pallas_call(copies_kernel, out_shape=[jax.ShapeDtypeStruct(shape, jnp....  1.78 us
  transfers between devices with their start and end apart: 10, of which 5 were waited for; matrix products, arithmetic and copies ran while one was open for 4% of the time, Pallas kernels for 0%

profile of v8, /device:TPU:384, one launch (start us, length us, event | category | flops | bytes accessed | tf_op | source)
XLA Modules:
  0.0 81.0 jit_solution(1076058270951914627)
XLA Ops:
  0.0 1.8 %copies.1 = (f32[8,64,256]{2,1,0:T(8,128)}, f32[64,256]{1,0:T(8,128)}) custom-call(s32[1]{0:T(128)} %bitcast.1.start_ref, f32[4,1,256,2,1,256]{5,4,3,2,1,0:T(1,128)} %window_ref.1), custom_call_target="tpu_custom_call" | custom-call | tf_op jit(solution)/shard_map/copies/pallas_call | solution.py:215
  1.8 7.1 %all-to-all-start = ((f32[8,64,256]{2,1,0:T(8,128)}), f32[8,64,256]{2,1,0:T(8,128)S(1)}, u32[]{:S(2)}, u32[]{:S(2)}) async-start(f32[8,64,256]{2,1,0:T(8,128)} %get-tuple-element.9), calls=%async_computation | async-start | bytes 1048576 | tf_op jit(solution)/shard_map/all_to_all | solution.py:255
  8.9 3.9 %collective-permute-start.4 = (f32[64,256]{1,0:T(8,128)}, f32[64,256]{1,0:T(8,128)S(1)}, u32[]{:S(2)}, u32[]{:S(2)}) collective-permute-start(f32[64,256]{1,0:T(8,128)} %get-tuple-element.12), channel_id=1, source_target_pairs={{0,8},{8,0},{1,9},{9,1},{2,10},{10,2},{3,11},{11,3},{4,12},{12,4},... | collective-permute-start | bytes 196616 | tf_op jit(solution)/shard_map/ppermute | solution.py:258
  12.8 1.1 %constant_dynamic-slice_fusion = f32[4,1,32,2,1,256]{5,4,3,2,1,0:T(1,128)S(1)} fusion(f32[4,1,256,2,1,256]{5,4,3,2,1,0:T(1,128)} %window_ref.1, s32[]{:T(128)S(6)} %select_n.90), kind=kLoop, calls=%fused_computation.28 | loop fusion | bytes 524292 | tf_op jit(solution)/shard_map/dynamic_slice | solution.py:268
  14.0 12.4 %all-to-all-done = f32[8,64,256]{2,1,0:T(8,128)S(1)} async-done(((f32[8,64,256]{2,1,0:T(8,128)}), f32[8,64,256]{2,1,0:T(8,128)S(1)}, u32[]{:S(2)}, u32[]{:S(2)}) %all-to-all-start) | async-done | bytes 524320 | tf_op jit(solution)/shard_map/all_to_all | solution.py:255
  26.4 0.0 copy-start
  26.4 0.9 %broadcast_in_dim.57 = f32[4,2,64,256]{3,2,1,0:T(8,128)} broadcast(f32[2,64,256]{2,1,0:T(8,128)S(1)} %slice.8), dimensions={1,2,3} | broadcast | bytes 655360 | tf_op jit(solution)/shard_map/broadcast_in_dim | solution.py:230
  27.3 4.3 %all-to-all-start.1 = ((f32[4,2,64,256]{3,2,1,0:T(8,128)}), f32[4,2,64,256]{3,2,1,0:T(8,128)S(1)}, u32[]{:S(2)}, u32[]{:S(2)}) async-start(f32[4,2,64,256]{3,2,1,0:T(8,128)} %broadcast_in_dim.57), calls=%async_computation.1 | async-start | bytes 1048576 | tf_op jit(solution)/shard_map/all_to_all | solution.py:231
  31.6 0.1 iota_compare_fusion
  31.7 9.6 %all-to-all-done.1 = f32[4,2,64,256]{3,2,1,0:T(8,128)S(1)} async-done(((f32[4,2,64,256]{3,2,1,0:T(8,128)}), f32[4,2,64,256]{3,2,1,0:T(8,128)S(1)}, u32[]{:S(2)}, u32[]{:S(2)}) %all-to-all-start.1) | async-done | bytes 524320 | tf_op jit(solution)/shard_map/all_to_all | solution.py:231
  41.3 0.7 collective-permute-start
  42.0 0.0 collective-permute-done.4
  42.0 0.0 copy-done
  42.1 1.3 %collective-permute-start.5 = (f32[2,64,256]{2,1,0:T(8,128)S(1)}, f32[2,64,256]{2,1,0:T(8,128)S(1)}, u32[]{:S(2)}, u32[]{:S(2)}) collective-permute-start(f32[2,64,256]{2,1,0:T(8,128)S(1)} %pad_maximum_fusion.1), channel_id=1, source_target_pairs={{0,48},{8,24},{1,49},{9,25},{2,50},{10,26},{3,51},{11,27},{4,52},{... | collective-permute-start | bytes 393224 | tf_op jit(solution)/shard_map/ppermute | solution.py:261
  43.4 0.1 broadcast_compare_fusion.1
  43.5 0.0 collective-permute-done.other_ref
  43.5 1.3 %collective-permute-start.1 = (f32[128,256]{1,0:T(8,128)S(1)}, f32[128,256]{1,0:T(8,128)S(1)}, u32[]{:S(2)}, u32[]{:S(2)}) collective-permute-start(f32[128,256]{1,0:T(8,128)S(1)} %get-tuple-element.11), channel_id=1, source_target_pairs={{0,4},{1,5},{8,12},{9,13},{16,20},{17,21},{24,28},{25,29},{32,36},... | collective-permute-start | bytes 393224 | tf_op jit(solution)/shard_map/ppermute | solution.py:273
  44.8 1.1 %collective-permute-done.5 = f32[2,64,256]{2,1,0:T(8,128)S(1)} collective-permute-done((f32[2,64,256]{2,1,0:T(8,128)S(1)}, f32[2,64,256]{2,1,0:T(8,128)S(1)}, u32[]{:S(2)}, u32[]{:S(2)}) %collective-permute-start.5) | collective-permute-done | bytes 131104 | tf_op jit(solution)/shard_map/ppermute | solution.py:261
  45.9 1.3 %collective-permute-start.6 = (f32[2,64,256]{2,1,0:T(8,128)S(1)}, f32[2,64,256]{2,1,0:T(8,128)S(1)}, u32[]{:S(2)}, u32[]{:S(2)}) collective-permute-start(f32[2,64,256]{2,1,0:T(8,128)S(1)} %broadcast_select_fusion), channel_id=1, source_target_pairs={{0,56},{8,16},{48,40},{24,32},{1,57},{9,17},{49,41},{25,33},{2,58}... | collective-permute-start | bytes 393224 | tf_op jit(solution)/shard_map/ppermute | solution.py:263
  47.2 16.5 %collective-permute-done.1 = f32[128,256]{1,0:T(8,128)S(1)} collective-permute-done((f32[128,256]{1,0:T(8,128)S(1)}, f32[128,256]{1,0:T(8,128)S(1)}, u32[]{:S(2)}, u32[]{:S(2)}) %collective-permute-start.1) | collective-permute-done | bytes 131104 | tf_op jit(solution)/shard_map/ppermute | solution.py:273
  63.7 1.3 %collective-permute-start.2 = (f32[128,256]{1,0:T(8,128)S(1)}, f32[128,256]{1,0:T(8,128)S(1)}, u32[]{:S(2)}, u32[]{:S(2)}) collective-permute-start(f32[128,256]{1,0:T(8,128)S(1)} %broadcast_select_fusion.2), channel_id=1, source_target_pairs={{0,2},{1,3},{4,6},{5,7},{8,10},{9,11},{12,14},{13,15},{16,18},{17,... | collective-permute-start | bytes 393224 | tf_op jit(solution)/shard_map/ppermute | solution.py:275
  65.0 0.0 collective-permute-done.6
  65.1 0.8 %broadcast_in_dim.62 = f32[4,2,64,256]{3,2,1,0:T(8,128)} broadcast(f32[2,64,256]{2,1,0:T(8,128)S(1)} %broadcast_select_fusion.1), dimensions={1,2,3} | broadcast | bytes 655360 | tf_op jit(solution)/shard_map/broadcast_in_dim | solution.py:230
  65.9 3.5 %all-to-all-start.2 = ((f32[4,2,64,256]{3,2,1,0:T(8,128)}), f32[4,2,64,256]{3,2,1,0:T(8,128)S(1)}, u32[]{:S(2)}, u32[]{:S(2)}) async-start(f32[4,2,64,256]{3,2,1,0:T(8,128)} %broadcast_in_dim.62), calls=%async_computation.2 | async-start | bytes 1048576 | tf_op jit(solution)/shard_map/all_to_all | solution.py:231
  69.4 0.0 collective-permute-done.2
  69.4 1.9 %collective-permute-start.3 = (f32[128,256]{1,0:T(8,128)S(1)}, f32[128,256]{1,0:T(8,128)S(1)}, u32[]{:S(2)}, u32[]{:S(2)}) collective-permute-start(f32[128,256]{1,0:T(8,128)S(1)} %broadcast_select_fusion.3), channel_id=1, source_target_pairs={{0,1},{1,0},{2,3},{3,2},{4,5},{5,4},{6,7},{7,6},{8,9},{9,8},{10,11... | collective-permute-start | bytes 393224 | tf_op jit(solution)/shard_map/ppermute | solution.py:277
  71.4 7.4 %all-to-all-done.2 = f32[4,2,64,256]{3,2,1,0:T(8,128)S(1)} async-done(((f32[4,2,64,256]{3,2,1,0:T(8,128)}), f32[4,2,64,256]{3,2,1,0:T(8,128)S(1)}, u32[]{:S(2)}, u32[]{:S(2)}) %all-to-all-start.2) | async-done | bytes 524320 | tf_op jit(solution)/shard_map/all_to_all | solution.py:231
  78.9 0.0 collective-permute-done.3
  78.9 0.7 fusion
  79.7 0.2 reshape.135
  79.8 0.2 fusion.8
  80.0 1.0 %copy.10 = f32[4,1,32,2,1,256]{5,4,3,2,1,0:T(1,128)} copy(f32[4,1,32,2,1,256]{5,2,4,3,1,0:T(8,128)S(1)} %fusion.8) | data formatting | bytes 524288 | tf_op jit(solution)/shard_map/jit(_where)/select_n | solution.py:293
  (19 shorter events, 0.3 us)
Async XLA Ops:
  1.8 24.6 %all-to-all-start = ((f32[8,64,256]{2,1,0:T(8,128)}), f32[8,64,256]{2,1,0:T(8,128)S(1)}, u32[]{:S(2)}, u32[]{:S(2)}) async-start(f32[8,64,256]{2,1,0:T(8,128)} %get-tuple-element.9), calls=%async_computation | async-start | bytes 1048576 | tf_op jit(solution)/shard_map/all_to_all | solution.py:255
  8.9 33.1 %collective-permute-start.4 = (f32[64,256]{1,0:T(8,128)}, f32[64,256]{1,0:T(8,128)S(1)}, u32[]{:S(2)}, u32[]{:S(2)}) collective-permute-start(f32[64,256]{1,0:T(8,128)} %get-tuple-element.12), channel_id=1, source_target_pairs={{0,8},{8,0},{1,9},{9,1},{2,10},{10,2},{3,11},{11,3},{4,12},{12,4},... | collective-permute-start | bytes 196616 | tf_op jit(solution)/shard_map/ppermute | solution.py:258
  26.4 15.6 %copy-start = (f32[64,256]{1,0:T(8,128)S(1)}, f32[64,256]{1,0:T(8,128)}, u32[]{:S(2)}) copy-start(f32[64,256]{1,0:T(8,128)} %get-tuple-element.12) | copy-start | bytes 196612
  27.3 14.0 %all-to-all-start.1 = ((f32[4,2,64,256]{3,2,1,0:T(8,128)}), f32[4,2,64,256]{3,2,1,0:T(8,128)S(1)}, u32[]{:S(2)}, u32[]{:S(2)}) async-start(f32[4,2,64,256]{3,2,1,0:T(8,128)} %broadcast_in_dim.57), calls=%async_computation.1 | async-start | bytes 1048576 | tf_op jit(solution)/shard_map/all_to_all | solution.py:231
  41.3 2.2 %collective-permute-start = (f32[640,256]{1,0:T(8,128)S(1)}, f32[640,256]{1,0:T(8,128)S(1)}, u32[]{:S(2)}, u32[]{:S(2)}) collective-permute-start(f32[640,256]{1,0:T(8,128)S(1)} %pad_maximum_fusion.mine_ref), channel_id=1, source_target_pairs={{0,1},{1,0},{8,9},{9,8},{16,17},{17,16},{24,25},{25,24},{32,33},{3... | collective-permute-start | bytes 1966088 | tf_op jit(solution)/shard_map/ppermute | solution.py:271
  42.1 3.8 %collective-permute-start.5 = (f32[2,64,256]{2,1,0:T(8,128)S(1)}, f32[2,64,256]{2,1,0:T(8,128)S(1)}, u32[]{:S(2)}, u32[]{:S(2)}) collective-permute-start(f32[2,64,256]{2,1,0:T(8,128)S(1)} %pad_maximum_fusion.1), channel_id=1, source_target_pairs={{0,48},{8,24},{1,49},{9,25},{2,50},{10,26},{3,51},{11,27},{4,52},{... | collective-permute-start | bytes 393224 | tf_op jit(solution)/shard_map/ppermute | solution.py:261
  43.5 20.2 %collective-permute-start.1 = (f32[128,256]{1,0:T(8,128)S(1)}, f32[128,256]{1,0:T(8,128)S(1)}, u32[]{:S(2)}, u32[]{:S(2)}) collective-permute-start(f32[128,256]{1,0:T(8,128)S(1)} %get-tuple-element.11), channel_id=1, source_target_pairs={{0,4},{1,5},{8,12},{9,13},{16,20},{17,21},{24,28},{25,29},{32,36},... | collective-permute-start | bytes 393224 | tf_op jit(solution)/shard_map/ppermute | solution.py:273
  45.9 19.1 %collective-permute-start.6 = (f32[2,64,256]{2,1,0:T(8,128)S(1)}, f32[2,64,256]{2,1,0:T(8,128)S(1)}, u32[]{:S(2)}, u32[]{:S(2)}) collective-permute-start(f32[2,64,256]{2,1,0:T(8,128)S(1)} %broadcast_select_fusion), channel_id=1, source_target_pairs={{0,56},{8,16},{48,40},{24,32},{1,57},{9,17},{49,41},{25,33},{2,58}... | collective-permute-start | bytes 393224 | tf_op jit(solution)/shard_map/ppermute | solution.py:263
  63.7 5.7 %collective-permute-start.2 = (f32[128,256]{1,0:T(8,128)S(1)}, f32[128,256]{1,0:T(8,128)S(1)}, u32[]{:S(2)}, u32[]{:S(2)}) collective-permute-start(f32[128,256]{1,0:T(8,128)S(1)} %broadcast_select_fusion.2), channel_id=1, source_target_pairs={{0,2},{1,3},{4,6},{5,7},{8,10},{9,11},{12,14},{13,15},{16,18},{17,... | collective-permute-start | bytes 393224 | tf_op jit(solution)/shard_map/ppermute | solution.py:275
  65.9 12.9 %all-to-all-start.2 = ((f32[4,2,64,256]{3,2,1,0:T(8,128)}), f32[4,2,64,256]{3,2,1,0:T(8,128)S(1)}, u32[]{:S(2)}, u32[]{:S(2)}) async-start(f32[4,2,64,256]{3,2,1,0:T(8,128)} %broadcast_in_dim.62), calls=%async_computation.2 | async-start | bytes 1048576 | tf_op jit(solution)/shard_map/all_to_all | solution.py:231
  69.4 9.5 %collective-permute-start.3 = (f32[128,256]{1,0:T(8,128)S(1)}, f32[128,256]{1,0:T(8,128)S(1)}, u32[]{:S(2)}, u32[]{:S(2)}) collective-permute-start(f32[128,256]{1,0:T(8,128)S(1)} %broadcast_select_fusion.3), channel_id=1, source_target_pairs={{0,1},{1,0},{2,3},{3,2},{4,5},{5,4},{6,7},{7,6},{8,9},{9,8},{10,11... | collective-permute-start | bytes 393224 | tf_op jit(solution)/shard_map/ppermute | solution.py:277
